TPU v7x, 256 devices: a whole 4x4x8 slice. The times are simulated.
256 devices in a mesh: gx: 32 (over z_lo, x, core), gy: 8 (over z_hi, y).
Axes of the slice: x: 4, y: 4, z: 8 (z_hi: 2, z_lo: 4; z = z_hi * 4 + z_lo), core: 2. Of those that a mesh axis runs over, the one named last changes fastest.
Arguments:
- right_side: float32 [512, 1024, 128], P('gx', 'gy'), may hold values from -50 to 50
- conductivity: float32 [512, 1024, 128], P('gx', 'gy'), may hold values from 0.2 to 5
Outputs:
- solution_field: float32 [512, 1024, 128], P('gx', 'gy')
- residual: float32 [512, 1024, 128], P('gx', 'gy')
All inputs are finite; a program needn't handle non-finite values.
Results may differ from a plain program's by a relative error of at most 0.0085.
Values sent between devices are 32-bit elements; how exact they have to be, the bound alone decides.
A program may use at most 64 MiB of HBM per device.

v0:
```python
import jax
import jax.numpy as jnp
from jax import lax
from jax.sharding import PartitionSpec as P

MARGIN = 4
SWEEPS = 3
ITERS = 2


absorb = 0.05
theta = 1.05
delta = 0.95


def with_halo(block, sides, width):
    for axis, dim in sides:
        count = lax.axis_size(axis)
        forward = [(i, i + 1) for i in range(count - 1)]
        backward = [(target, source) for source, target in forward]
        low = lax.ppermute(
            lax.slice_in_dim(block, block.shape[dim] - width, None, axis=dim), axis, forward
        )
        high = lax.ppermute(lax.slice_in_dim(block, 0, width, axis=dim), axis, backward)
        block = jnp.concatenate([low, block, high], axis=dim)
    return block


def from_behind(x, axis, by):
    size = lax.axis_size(axis)
    pairs = [(i, i + by) for i in range(size) if 0 <= i + by < size]
    return lax.ppermute(x, axis, pairs)


def coefficients(wide):
    padded = jnp.pad(wide, ((0, 0), (0, 0), (1, 1)))
    center = padded[1:-1, 1:-1, 1:-1]
    diagonal = absorb + jnp.zeros_like(center)
    for beside in (
        padded[:-2, 1:-1, 1:-1],
        padded[2:, 1:-1, 1:-1],
        padded[1:-1, :-2, 1:-1],
        padded[1:-1, 2:, 1:-1],
        padded[1:-1, 1:-1, :-2],
        padded[1:-1, 1:-1, 2:],
    ):
        diagonal = diagonal + jnp.where(beside > 0, 0.5 * (center + beside), center)
    living = center > 0
    face_x = jnp.where(living[1:] & living[:-1], 0.5 * (center[1:] + center[:-1]), 0.0)
    face_y = jnp.where(living[:, 1:] & living[:, :-1], 0.5 * (center[:, 1:] + center[:, :-1]), 0.0)
    face_z = jnp.where(
        living[:, :, 1:] & living[:, :, :-1], 0.5 * (center[:, :, 1:] + center[:, :, :-1]), 0.0
    )
    return (diagonal, face_x, face_y, face_z)


def local_apply(field, coeffs):
    diagonal, face_x, face_y, face_z = coeffs
    beside = jnp.pad(face_x * field[1:], ((0, 1), (0, 0), (0, 0))) + jnp.pad(
        face_x * field[:-1], ((1, 0), (0, 0), (0, 0))
    )
    beside = (
        beside
        + jnp.pad(face_y * field[:, 1:], ((0, 0), (0, 1), (0, 0)))
        + jnp.pad(face_y * field[:, :-1], ((0, 0), (1, 0), (0, 0)))
    )
    beside = (
        beside
        + jnp.pad(face_z * field[:, :, 1:], ((0, 0), (0, 0), (0, 1)))
        + jnp.pad(face_z * field[:, :, :-1], ((0, 0), (0, 0), (1, 0)))
    )
    return diagonal * field - beside


def chebyshev(source, coeffs):
    inverse = 1.0 / coeffs[0]
    ratio_sig = theta / delta
    ratio_now = 1.0 / ratio_sig
    update = inverse * source / theta
    answer = update
    for sweep in range(SWEEPS - 1):
        ratio_new = 1.0 / (2.0 * ratio_sig - ratio_now)
        update = ratio_new * ratio_now * update + 2.0 * ratio_new / delta * inverse * (
            source - local_apply(answer, coeffs)
        )
        answer = answer + update
        ratio_now = ratio_new
    return answer


def operate_brick(field, coeffs):
    width = field.shape[0]
    depth = field.shape[1]
    with_rim = with_halo(field, (("gx", 0), ("gy", 1)), 1)
    diagonal, face_x, face_y, face_z = coeffs
    edge = MARGIN
    faces_x = face_x[edge - 1 : width + edge, edge : depth + edge]
    faces_y = face_y[edge : width + edge, edge - 1 : depth + edge]
    faces_z = face_z[edge : width + edge, edge : depth + edge]
    diag_brick = diagonal[edge : width + edge, edge : depth + edge]
    along_x = with_rim[:, 1:-1]
    beside = faces_x[1:] * along_x[2:] + faces_x[:-1] * along_x[:-2]
    along_y = with_rim[1:-1]
    beside = beside + faces_y[:, 1:] * along_y[:, 2:] + faces_y[:, :-1] * along_y[:, :-2]
    beside = (
        beside
        + jnp.pad(faces_z * field[:, :, 1:], ((0, 0), (0, 0), (0, 1)))
        + jnp.pad(faces_z * field[:, :, :-1], ((0, 0), (0, 0), (1, 0)))
    )
    return diag_brick * field - beside


def give_back(extended):
    edge = MARGIN
    size_x = extended.shape[0] - 2 * edge
    from_high = from_behind(extended[:edge], "gx", -1)
    from_low = from_behind(extended[size_x + edge :], "gx", 1)
    middle = (
        extended[edge : size_x + edge].at[:edge].add(from_low).at[size_x - edge :].add(from_high)
    )
    size_y = middle.shape[1] - 2 * edge
    from_high = from_behind(middle[:, :edge], "gy", -1)
    from_low = from_behind(middle[:, size_y + edge :], "gy", 1)
    return (
        middle[:, edge : size_y + edge]
        .at[:, :edge]
        .add(from_low)
        .at[:, size_y - edge :]
        .add(from_high)
    )


def precond_sum(residue, smoothed):
    return lax.psum(jnp.sum(residue * smoothed), ("gx", "gy"))


def shards(right_side, conductivity):
    wide = with_halo(conductivity, (("gx", 0), ("gy", 1)), MARGIN + 1)
    coeffs = coefficients(wide)

    def smooth(residue):
        padded = with_halo(residue, (("gx", 0), ("gy", 1)), MARGIN)
        return give_back(chebyshev(padded, coeffs))

    solution_field = jnp.zeros_like(right_side)
    residual = right_side
    precond = smooth(residual)
    direction = precond
    dot_now = precond_sum(residual, precond)
    for step in range(ITERS):
        image = operate_brick(direction, coeffs)
        step_size = dot_now / lax.psum(jnp.sum(direction * image), ("gx", "gy"))
        solution_field = solution_field + step_size * direction
        residual = residual - step_size * image
        if step + 1 < ITERS:
            precond = smooth(residual)
            dot_next = precond_sum(residual, precond)
            direction = precond + dot_next / dot_now * direction
            dot_now = dot_next
    return (solution_field, residual)


def solution(mesh):
    in_specs = (P("gx", "gy", None), P("gx", "gy", None))
    out_specs = (P("gx", "gy", None), P("gx", "gy", None))
    return jax.shard_map(shards, mesh=mesh, in_specs=in_specs, out_specs=out_specs, check_vma=False)
```

profile of v0, /device:TPU:8, one launch (start us, length us, event | category | flops | bytes accessed | tf_op | source)
XLA Modules:
  0.0 454.3 jit_solution(2347227778427394391)
XLA Ops:
  1.8 1.8 collective-permute-start.4
  3.6 1.3 collective-permute-start.5
  6.0 1.3 collective-permute-start.1
  7.3 4.9 %collective-permute-start = (f32[5,128,128]{2,1,0:T(8,128)S(1)}, f32[5,128,128]{2,1,0:T(8,128)S(1)}, u32[]{:S(2)}, u32[]{:S(2)}) collective-permute-start(f32[5,128,128]{2,1,0:T(8,128)S(1)} %get-tuple-element.164), channel_id=1, source_target_pairs={{0,8},{8,16},{16,24},{24,32},{32,40},{40,48},{48,56},{56,64},{64,7... | collective-permute-start | bytes 983048 | tf_op jit(solution)/shard_map/ppermute | solution.py:21
  13.7 3.5 collective-permute-start.2
  17.2 2.4 collective-permute-start.3
  19.6 3.5 collective-permute-start.6
  23.1 2.4 collective-permute-start.7
  26.0 7.2 %collective-permute-done.7 = f32[24,4,128]{2,1,0:T(4,128)S(1)} collective-permute-done((f32[24,4,128]{2,1,0:T(4,128)S(1)}, f32[24,4,128]{2,1,0:T(4,128)S(1)}, u32[]{:S(2)}, u32[]{:S(2)}) %collective-permute-start.7) | collective-permute-done | bytes 49184 | tf_op jit(solution)/shard_map/ppermute | solution.py:24
  33.1 2.8 broadcast_multiply_fusion.1
  36.4 1.4 slice_multiply_fusion.13
  39.5 1.6 fusion.34
  42.2 1.7 add_add_fusion.1
  43.9 5.0 %collective-permute-start.8 = (f32[4,136,128]{2,1,0:T(8,128)S(1)}, f32[4,136,128]{2,1,0:T(8,128)S(1)}, u32[]{:S(2)}, u32[]{:S(2)}) collective-permute-start(f32[4,136,128]{2,1,0:T(8,128)S(1)} %get-tuple-element.144), channel_id=1, source_target_pairs={{0,8},{8,16},{16,24},{24,32},{32,40},{40,48},{48,56},{56,64},{64,7... | collective-permute-start | bytes 835592 | tf_op jit(solution)/shard_map/ppermute | solution.py:32
  48.9 1.3 collective-permute-start.9
  50.3 5.4 %collective-permute-done.9 = f32[4,136,128]{2,1,0:T(8,128)S(1)} collective-permute-done((f32[4,136,128]{2,1,0:T(8,128)S(1)}, f32[4,136,128]{2,1,0:T(8,128)S(1)}, u32[]{:S(2)}, u32[]{:S(2)}) %collective-permute-start.9) | collective-permute-done | bytes 278560 | tf_op jit(solution)/shard_map/ppermute | solution.py:32
  55.8 9.9 %collective-permute-start.10 = (f32[16,4,128]{2,1,0:T(4,128)S(1)}, f32[16,4,128]{2,1,0:T(4,128)S(1)}, u32[]{:S(2)}, u32[]{:S(2)}) collective-permute-start(f32[16,4,128]{2,1,0:T(4,128)S(1)} %get-tuple-element.156), channel_id=1, source_target_pairs={{0,1},{1,2},{2,3},{3,4},{4,5},{5,6},{6,7},{8,9},{9,10},{10,11},{11... | collective-permute-start | bytes 98312 | tf_op jit(solution)/shard_map/ppermute | solution.py:32
  65.9 1.9 collective-permute-start.11
  67.8 9.9 %collective-permute-done.11 = f32[16,4,128]{2,1,0:T(4,128)S(1)} collective-permute-done((f32[16,4,128]{2,1,0:T(4,128)S(1)}, f32[16,4,128]{2,1,0:T(4,128)S(1)}, u32[]{:S(2)}, u32[]{:S(2)}) %collective-permute-start.11) | collective-permute-done | bytes 32800 | tf_op jit(solution)/shard_map/ppermute | solution.py:32
  77.8 5.7 %collective-permute-start.13 = (f32[1,128,128]{2,1,0:T(8,128)S(1)}, f32[1,128,128]{2,1,0:T(8,128)S(1)}, u32[]{:S(2)}, u32[]{:S(2)}) collective-permute-start(f32[1,128,128]{2,1,0:T(8,128)S(1)} %get-tuple-element.161), channel_id=1, source_target_pairs={{0,8},{8,16},{16,24},{24,32},{32,40},{40,48},{48,56},{56,64},{64,7... | collective-permute-start | bytes 196616 | tf_op jit(solution)/shard_map/ppermute | solution.py:21
  84.8 2.3 collective-permute-done.12
  87.1 1.9 collective-permute-start.14
  89.1 3.9 collective-permute-start.15
  94.6 3.8 multiply_reduce_fusion.2
  98.5 99.3 %all-reduce.29 = (f32[]{:T(128)}, f32[]{:T(128)}) all-reduce(f32[]{:T(128)} %get-tuple-element.99, f32[]{:T(128)} %get-tuple-element.98), channel_id=1, replica_groups=mesh['gx'=32,'gy'=8] {'gx','gy'}, use_global_device_ids=true, to_apply=%region_1.2 | all-reduce | flops 2 | bytes 16 | tf_op jit(solution)/shard_map/psum | solution.py:134
  199.1 1.7 multiply_subtract_fusion.1
  200.8 2.1 collective-permute-start.16
  204.2 2.1 collective-permute-done.17
  206.3 3.4 collective-permute-start.18
  209.7 2.4 collective-permute-start.19
  212.3 3.4 collective-permute-done.19
  218.4 2.2 fusion.35
  221.9 2.3 add_add_fusion
  224.2 5.3 %collective-permute-start.20 = (f32[4,136,128]{2,1,0:T(8,128)S(1)}, f32[4,136,128]{2,1,0:T(8,128)S(1)}, u32[]{:S(2)}, u32[]{:S(2)}) collective-permute-start(f32[4,136,128]{2,1,0:T(8,128)S(1)} %get-tuple-element.142), channel_id=1, source_target_pairs={{0,8},{8,16},{16,24},{24,32},{32,40},{40,48},{48,56},{56,64},{64,7... | collective-permute-start | bytes 835592 | tf_op jit(solution)/shard_map/ppermute | solution.py:32
  230.9 2.8 collective-permute-done.21
  233.7 6.0 %collective-permute-start.22 = (f32[16,4,128]{2,1,0:T(4,128)S(1)}, f32[16,4,128]{2,1,0:T(4,128)S(1)}, u32[]{:S(2)}, u32[]{:S(2)}) collective-permute-start(f32[16,4,128]{2,1,0:T(4,128)S(1)} %get-tuple-element.154), channel_id=1, source_target_pairs={{0,1},{1,2},{2,3},{3,4},{4,5},{5,6},{6,7},{8,9},{9,10},{10,11},{11... | collective-permute-start | bytes 98312 | tf_op jit(solution)/shard_map/ppermute | solution.py:32
  239.8 1.9 collective-permute-start.23
  241.8 9.9 %collective-permute-done.23 = f32[16,4,128]{2,1,0:T(4,128)S(1)} collective-permute-done((f32[16,4,128]{2,1,0:T(4,128)S(1)}, f32[16,4,128]{2,1,0:T(4,128)S(1)}, u32[]{:S(2)}, u32[]{:S(2)}) %collective-permute-start.23) | collective-permute-done | bytes 32800 | tf_op jit(solution)/shard_map/ppermute | solution.py:32
  253.6 87.8 %psum.30 = f32[]{:T(128)} all-reduce(f32[]{:T(128)} %multiply_reduce_fusion.1), channel_id=1, replica_groups=mesh['gx'=32,'gy'=8] {'gx','gy'}, use_global_device_ids=true, to_apply=%region_5.6 | all-reduce | flops 1 | bytes 8 | tf_op jit(solution)/shard_map/psum | solution.py:134
  342.7 1.8 multiply_add_fusion.3
  344.5 1.8 collective-permute-start.25
  347.7 2.8 collective-permute-done.24
  350.5 3.7 collective-permute-start.26
  354.3 2.3 collective-permute-start.27
  357.1 2.9 collective-permute-done.27
  359.9 3.8 multiply_reduce_fusion
  363.7 85.3 %psum.31 = f32[]{:T(128)} all-reduce(f32[]{:T(128)} %get-tuple-element.102), channel_id=1, replica_groups=mesh['gx'=32,'gy'=8] {'gx','gy'}, use_global_device_ids=true, to_apply=%region_7.8 | all-reduce | flops 1 | bytes 8 | tf_op jit(solution)/shard_map/psum | solution.py:152
  450.4 4.0 multiply_subtract_fusion
  (98 shorter events, 21.4 us)
Async XLA Ops:
  0.6 11.7 %copy-start.9 = (f32[16,128,128]{2,1,0:T(8,128)S(1)}, f32[16,128,128]{2,1,0:T(8,128)}, u32[]{:S(2)}) copy-start(f32[16,128,128]{2,1,0:T(8,128)} %param.18) | copy-start | bytes 3145732
  1.8 10.4 %collective-permute-start.4 = (f32[4,128,128]{2,1,0:T(8,128)S(1)}, f32[4,128,128]{2,1,0:T(8,128)S(1)}, u32[]{:S(2)}, u32[]{:S(2)}) collective-permute-start(f32[4,128,128]{2,1,0:T(8,128)S(1)} %get-tuple-element.166), channel_id=1, source_target_pairs={{0,8},{8,16},{16,24},{24,32},{32,40},{40,48},{48,56},{56,64},{64,7... | collective-permute-start | bytes 786440 | tf_op jit(solution)/shard_map/ppermute | solution.py:21
  3.6 8.8 %collective-permute-start.5 = (f32[4,128,128]{2,1,0:T(8,128)S(1)}, f32[4,128,128]{2,1,0:T(8,128)S(1)}, u32[]{:S(2)}, u32[]{:S(2)}) collective-permute-start(f32[4,128,128]{2,1,0:T(8,128)S(1)} %get-tuple-element.165), channel_id=1, source_target_pairs={{8,0},{16,8},{24,16},{32,24},{40,32},{48,40},{56,48},{64,56},{72,6... | collective-permute-start | bytes 786440 | tf_op jit(solution)/shard_map/ppermute | solution.py:24
  6.0 7.6 %collective-permute-start.1 = (f32[5,128,128]{2,1,0:T(8,128)S(1)}, f32[5,128,128]{2,1,0:T(8,128)S(1)}, u32[]{:S(2)}, u32[]{:S(2)}) collective-permute-start(f32[5,128,128]{2,1,0:T(8,128)S(1)} %get-tuple-element.163), channel_id=1, source_target_pairs={{8,0},{16,8},{24,16},{32,24},{40,32},{48,40},{56,48},{64,56},{72,6... | collective-permute-start | bytes 983048 | tf_op jit(solution)/shard_map/ppermute | solution.py:24
  7.3 6.2 %collective-permute-start = (f32[5,128,128]{2,1,0:T(8,128)S(1)}, f32[5,128,128]{2,1,0:T(8,128)S(1)}, u32[]{:S(2)}, u32[]{:S(2)}) collective-permute-start(f32[5,128,128]{2,1,0:T(8,128)S(1)} %get-tuple-element.164), channel_id=1, source_target_pairs={{0,8},{8,16},{16,24},{24,32},{32,40},{40,48},{48,56},{56,64},{64,7... | collective-permute-start | bytes 983048 | tf_op jit(solution)/shard_map/ppermute | solution.py:21
  12.3 1.2 copy-start.11
  13.7 11.7 %collective-permute-start.2 = (f32[26,5,128]{2,1,0:T(8,128)S(1)}, f32[26,5,128]{2,1,0:T(8,128)S(1)}, u32[]{:S(2)}, u32[]{:S(2)}) collective-permute-start(f32[26,5,128]{2,1,0:T(8,128)S(1)} %get-tuple-element.139), channel_id=1, source_target_pairs={{0,1},{1,2},{2,3},{3,4},{4,5},{5,6},{6,7},{8,9},{9,10},{10,11},{11... | collective-permute-start | bytes 199688 | tf_op jit(solution)/shard_map/ppermute | solution.py:21
  17.2 8.3 %collective-permute-start.3 = (f32[26,5,128]{2,1,0:T(8,128)S(1)}, f32[26,5,128]{2,1,0:T(8,128)S(1)}, u32[]{:S(2)}, u32[]{:S(2)}) collective-permute-start(f32[26,5,128]{2,1,0:T(8,128)S(1)} %get-tuple-element.140), channel_id=1, source_target_pairs={{1,0},{2,1},{3,2},{4,3},{5,4},{6,5},{7,6},{9,8},{10,9},{11,10},{12... | collective-permute-start | bytes 199688 | tf_op jit(solution)/shard_map/ppermute | solution.py:24
  19.6 6.4 %collective-permute-start.6 = (f32[24,4,128]{2,1,0:T(4,128)S(1)}, f32[24,4,128]{2,1,0:T(4,128)S(1)}, u32[]{:S(2)}, u32[]{:S(2)}) collective-permute-start(f32[24,4,128]{2,1,0:T(4,128)S(1)} %get-tuple-element.147), channel_id=1, source_target_pairs={{0,1},{1,2},{2,3},{3,4},{4,5},{5,6},{6,7},{8,9},{9,10},{10,11},{11... | collective-permute-start | bytes 147464 | tf_op jit(solution)/shard_map/ppermute | solution.py:21
  23.1 10.1 %collective-permute-start.7 = (f32[24,4,128]{2,1,0:T(4,128)S(1)}, f32[24,4,128]{2,1,0:T(4,128)S(1)}, u32[]{:S(2)}, u32[]{:S(2)}) collective-permute-start(f32[24,4,128]{2,1,0:T(4,128)S(1)} %get-tuple-element.148), channel_id=1, source_target_pairs={{1,0},{2,1},{3,2},{4,3},{5,4},{6,5},{7,6},{9,8},{10,9},{11,10},{12... | collective-permute-start | bytes 147464 | tf_op jit(solution)/shard_map/ppermute | solution.py:24
  35.9 58.7 %copy-start = (f32[24,136,128]{2,1,0:T(8,128)}, f32[24,136,128]{2,1,0:T(8,128)S(1)}, u32[]{:S(2)}) copy-start(f32[24,136,128]{2,1,0:T(8,128)S(1)} %get-tuple-element.116) | copy-start | bytes 5013508
  37.8 55.2 %copy-start.3 = (f32[24,136,127]{2,1,0:T(8,128)}, f32[24,136,127]{2,1,0:T(8,128)S(1)}, u32[]{:S(2)}) copy-start(f32[24,136,127]{2,1,0:T(8,128)S(1)} %get-tuple-element.114) | copy-start | bytes 4974340
  43.9 6.4 %collective-permute-start.8 = (f32[4,136,128]{2,1,0:T(8,128)S(1)}, f32[4,136,128]{2,1,0:T(8,128)S(1)}, u32[]{:S(2)}, u32[]{:S(2)}) collective-permute-start(f32[4,136,128]{2,1,0:T(8,128)S(1)} %get-tuple-element.144), channel_id=1, source_target_pairs={{0,8},{8,16},{16,24},{24,32},{32,40},{40,48},{48,56},{56,64},{64,7... | collective-permute-start | bytes 835592 | tf_op jit(solution)/shard_map/ppermute | solution.py:32
  48.9 6.9 %collective-permute-start.9 = (f32[4,136,128]{2,1,0:T(8,128)S(1)}, f32[4,136,128]{2,1,0:T(8,128)S(1)}, u32[]{:S(2)}, u32[]{:S(2)}) collective-permute-start(f32[4,136,128]{2,1,0:T(8,128)S(1)} %get-tuple-element.143), channel_id=1, source_target_pairs={{8,0},{16,8},{24,16},{32,24},{40,32},{48,40},{56,48},{64,56},{72,6... | collective-permute-start | bytes 835592 | tf_op jit(solution)/shard_map/ppermute | solution.py:32
  55.8 12.0 %collective-permute-start.10 = (f32[16,4,128]{2,1,0:T(4,128)S(1)}, f32[16,4,128]{2,1,0:T(4,128)S(1)}, u32[]{:S(2)}, u32[]{:S(2)}) collective-permute-start(f32[16,4,128]{2,1,0:T(4,128)S(1)} %get-tuple-element.156), channel_id=1, source_target_pairs={{0,1},{1,2},{2,3},{3,4},{4,5},{5,6},{6,7},{8,9},{9,10},{10,11},{11... | collective-permute-start | bytes 98312 | tf_op jit(solution)/shard_map/ppermute | solution.py:32
  65.9 11.9 %collective-permute-start.11 = (f32[16,4,128]{2,1,0:T(4,128)S(1)}, f32[16,4,128]{2,1,0:T(4,128)S(1)}, u32[]{:S(2)}, u32[]{:S(2)}) collective-permute-start(f32[16,4,128]{2,1,0:T(4,128)S(1)} %get-tuple-element.155), channel_id=1, source_target_pairs={{1,0},{2,1},{3,2},{4,3},{5,4},{6,5},{7,6},{9,8},{10,9},{11,10},{12... | collective-permute-start | bytes 98312 | tf_op jit(solution)/shard_map/ppermute | solution.py:32
  77.8 16.9 %copy-start.7 = (f32[16,128,128]{2,1,0:T(8,128)}, f32[16,128,128]{2,1,0:T(8,128)S(1)}, u32[]{:S(2)}) copy-start(f32[16,128,128]{2,1,0:T(8,128)S(1)} %fusion.32) | copy-start | bytes 3145732
  77.8 7.0 %collective-permute-start.13 = (f32[1,128,128]{2,1,0:T(8,128)S(1)}, f32[1,128,128]{2,1,0:T(8,128)S(1)}, u32[]{:S(2)}, u32[]{:S(2)}) collective-permute-start(f32[1,128,128]{2,1,0:T(8,128)S(1)} %get-tuple-element.161), channel_id=1, source_target_pairs={{0,8},{8,16},{16,24},{24,32},{32,40},{40,48},{48,56},{56,64},{64,7... | collective-permute-start | bytes 196616 | tf_op jit(solution)/shard_map/ppermute | solution.py:21
  83.5 3.6 collective-permute-start.12
  87.1 6.4 %collective-permute-start.14 = (f32[18,1,128]{2,1,0:T(1,128)S(1)}, f32[18,1,128]{2,1,0:T(1,128)S(1)}, u32[]{:S(2)}, u32[]{:S(2)}) collective-permute-start(f32[18,1,128]{2,1,0:T(1,128)S(1)} %get-tuple-element.151), channel_id=1, source_target_pairs={{1,0},{2,1},{3,2},{4,3},{5,4},{6,5},{7,6},{9,8},{10,9},{11,10},{12... | collective-permute-start | bytes 27656 | tf_op jit(solution)/shard_map/ppermute | solution.py:24
  89.1 5.6 %collective-permute-start.15 = (f32[18,1,128]{2,1,0:T(1,128)S(1)}, f32[18,1,128]{2,1,0:T(1,128)S(1)}, u32[]{:S(2)}, u32[]{:S(2)}) collective-permute-start(f32[18,1,128]{2,1,0:T(1,128)S(1)} %get-tuple-element.152), channel_id=1, source_target_pairs={{0,1},{1,2},{2,3},{3,4},{4,5},{5,6},{6,7},{8,9},{9,10},{10,11},{11... | collective-permute-start | bytes 27656 | tf_op jit(solution)/shard_map/ppermute | solution.py:21
  200.7 50.9 %copy-start.6 = (f32[16,128,128]{2,1,0:T(8,128)}, f32[16,128,128]{2,1,0:T(8,128)S(1)}, u32[]{:S(2)}) copy-start(f32[16,128,128]{2,1,0:T(8,128)S(1)} %multiply_subtract_fusion.1) | copy-start | bytes 3145732
  200.7 15.0 %copy-start.1 = (f32[24,136,128]{2,1,0:T(8,128)S(1)}, f32[24,136,128]{2,1,0:T(8,128)}, u32[]{:S(2)}) copy-start(f32[24,136,128]{2,1,0:T(8,128)} %copy-done) | copy-start | bytes 5013508
  200.8 3.4 collective-permute-start.16
  202.9 3.4 collective-permute-start.17
  206.3 6.0 %collective-permute-start.18 = (f32[24,4,128]{2,1,0:T(4,128)S(1)}, f32[24,4,128]{2,1,0:T(4,128)S(1)}, u32[]{:S(2)}, u32[]{:S(2)}) collective-permute-start(f32[24,4,128]{2,1,0:T(4,128)S(1)} %get-tuple-element.145), channel_id=1, source_target_pairs={{0,1},{1,2},{2,3},{3,4},{4,5},{5,6},{6,7},{8,9},{9,10},{10,11},{11... | collective-permute-start | bytes 147464 | tf_op jit(solution)/shard_map/ppermute | solution.py:21
  209.7 6.0 %collective-permute-start.19 = (f32[24,4,128]{2,1,0:T(4,128)S(1)}, f32[24,4,128]{2,1,0:T(4,128)S(1)}, u32[]{:S(2)}, u32[]{:S(2)}) collective-permute-start(f32[24,4,128]{2,1,0:T(4,128)S(1)} %get-tuple-element.146), channel_id=1, source_target_pairs={{1,0},{2,1},{3,2},{4,3},{5,4},{6,5},{7,6},{9,8},{10,9},{11,10},{12... | collective-permute-start | bytes 147464 | tf_op jit(solution)/shard_map/ppermute | solution.py:24
  216.4 1.4 copy-start.4
  224.2 6.6 %collective-permute-start.20 = (f32[4,136,128]{2,1,0:T(8,128)S(1)}, f32[4,136,128]{2,1,0:T(8,128)S(1)}, u32[]{:S(2)}, u32[]{:S(2)}) collective-permute-start(f32[4,136,128]{2,1,0:T(8,128)S(1)} %get-tuple-element.142), channel_id=1, source_target_pairs={{0,8},{8,16},{16,24},{24,32},{32,40},{40,48},{48,56},{56,64},{64,7... | collective-permute-start | bytes 835592 | tf_op jit(solution)/shard_map/ppermute | solution.py:32
  229.5 4.2 collective-permute-start.21
  233.7 8.0 %collective-permute-start.22 = (f32[16,4,128]{2,1,0:T(4,128)S(1)}, f32[16,4,128]{2,1,0:T(4,128)S(1)}, u32[]{:S(2)}, u32[]{:S(2)}) collective-permute-start(f32[16,4,128]{2,1,0:T(4,128)S(1)} %get-tuple-element.154), channel_id=1, source_target_pairs={{0,1},{1,2},{2,3},{3,4},{4,5},{5,6},{6,7},{8,9},{9,10},{10,11},{11... | collective-permute-start | bytes 98312 | tf_op jit(solution)/shard_map/ppermute | solution.py:32
  239.8 11.8 %collective-permute-start.23 = (f32[16,4,128]{2,1,0:T(4,128)S(1)}, f32[16,4,128]{2,1,0:T(4,128)S(1)}, u32[]{:S(2)}, u32[]{:S(2)}) collective-permute-start(f32[16,4,128]{2,1,0:T(4,128)S(1)} %get-tuple-element.153), channel_id=1, source_target_pairs={{1,0},{2,1},{3,2},{4,3},{5,4},{6,5},{7,6},{9,8},{10,9},{11,10},{12... | collective-permute-start | bytes 98312 | tf_op jit(solution)/shard_map/ppermute | solution.py:32
  251.7 1.0 copy-start.10
  342.7 13.9 %copy-start.5 = (f32[24,136,127]{2,1,0:T(8,128)S(1)}, f32[24,136,127]{2,1,0:T(8,128)}, u32[]{:S(2)}) copy-start(f32[24,136,127]{2,1,0:T(8,128)} %copy-done.3) | copy-start | bytes 4974340
  344.5 15.5 %copy-start.8 = (f32[16,128,128]{2,1,0:T(8,128)}, f32[16,128,128]{2,1,0:T(8,128)S(1)}, u32[]{:S(2)}) copy-start(f32[16,128,128]{2,1,0:T(8,128)S(1)} %multiply_add_fusion.3) | copy-start | bytes 3145732
  344.5 3.1 collective-permute-start.25
  346.3 4.2 collective-permute-start.24
  350.5 6.5 %collective-permute-start.26 = (f32[18,1,128]{2,1,0:T(1,128)S(1)}, f32[18,1,128]{2,1,0:T(1,128)S(1)}, u32[]{:S(2)}, u32[]{:S(2)}) collective-permute-start(f32[18,1,128]{2,1,0:T(1,128)S(1)} %get-tuple-element.149), channel_id=1, source_target_pairs={{1,0},{2,1},{3,2},{4,3},{5,4},{6,5},{7,6},{9,8},{10,9},{11,10},{12... | collective-permute-start | bytes 27656 | tf_op jit(solution)/shard_map/ppermute | solution.py:24
  354.2 5.7 %copy-start.2 = (f32[24,136,128]{2,1,0:T(8,128)S(1)}, f32[24,136,128]{2,1,0:T(8,128)}, u32[]{:S(2)}) copy-start(f32[24,136,128]{2,1,0:T(8,128)} %copy-done) | copy-start | bytes 5013508
  354.3 5.7 %collective-permute-start.27 = (f32[18,1,128]{2,1,0:T(1,128)S(1)}, f32[18,1,128]{2,1,0:T(1,128)S(1)}, u32[]{:S(2)}, u32[]{:S(2)}) collective-permute-start(f32[18,1,128]{2,1,0:T(1,128)S(1)} %get-tuple-element.150), channel_id=1, source_target_pairs={{0,1},{1,2},{2,3},{3,4},{4,5},{5,6},{6,7},{8,9},{9,10},{10,11},{11... | collective-permute-start | bytes 27656 | tf_op jit(solution)/shard_map/ppermute | solution.py:21
where the time goes:
time: 457 us; the launch traced here: 454 us
  blocking collectives  272 us (60%)
  starting transfers between devices  84.6 us (19%)
  waiting for transfers between devices  51 us (11%)
  other arithmetic  35.5 us (8%)
  local copies, waits for them, and re-layouts  5.33 us (1%)
  between operations  5.33 us (1%)
    psum x2, blocking collectives, precond_sum(): return lax.psum(jnp.sum(residue * smoothed), ('gx', 'gy'))  187 us
    psum x1, blocking collectives, shards(): step_size = dot_now / lax.psum(jnp.sum(direction * image), ('gx', 'gy'))  85.3 us
    ppermute x10, starting transfers between devices, with_halo(): lax.ppermute(lax.slice_in_dim(block, block.shape[dim] - width, None, axis...  32.8 us
    ppermute x8, starting transfers between devices, from_behind(): return lax.ppermute(x, axis, pairs)  32.5 us
    ppermute x8, waiting for transfers between devices, from_behind(): return lax.ppermute(x, axis, pairs)  28 us
    ppermute x10, starting transfers between devices, with_halo(): lax.ppermute(lax.slice_in_dim(block, 0, width, axis=dim), axis, backward)  19.3 us
    ppermute x10, waiting for transfers between devices, with_halo(): lax.ppermute(lax.slice_in_dim(block, 0, width, axis=dim), axis, backward)  17.9 us
  transfers between devices with their start and end apart: 28, of which 13 were waited for; matrix products, arithmetic and copies ran while one was open for 1% of the time, Pallas kernels for 0%

commit v1 on v0

--- a/solution.py
+++ b/solution.py
@@ -130,10 +130,6 @@
     )
 
 
-def precond_sum(residue, smoothed):
-    return lax.psum(jnp.sum(residue * smoothed), ("gx", "gy"))
-
-
 def shards(right_side, conductivity):
     wide = with_halo(conductivity, (("gx", 0), ("gy", 1)), MARGIN + 1)
     coeffs = coefficients(wide)
@@ -142,22 +138,21 @@
         padded = with_halo(residue, (("gx", 0), ("gy", 1)), MARGIN)
         return give_back(chebyshev(padded, coeffs))
 
-    solution_field = jnp.zeros_like(right_side)
-    residual = right_side
-    precond = smooth(residual)
-    direction = precond
-    dot_now = precond_sum(residual, precond)
-    for step in range(ITERS):
-        image = operate_brick(direction, coeffs)
-        step_size = dot_now / lax.psum(jnp.sum(direction * image), ("gx", "gy"))
-        solution_field = solution_field + step_size * direction
-        residual = residual - step_size * image
-        if step + 1 < ITERS:
-            precond = smooth(residual)
-            dot_next = precond_sum(residual, precond)
-            direction = precond + dot_next / dot_now * direction
-            dot_now = dot_next
-    return (solution_field, residual)
+    z0 = smooth(right_side)
+    w0 = operate_brick(z0, coeffs)
+    z1 = smooth(w0)
+    w1 = operate_brick(z1, coeffs)
+    pairs = ((right_side, z0), (z0, w0), (right_side, z1), (w0, z1), (z0, w1), (z1, w1))
+    dots = lax.psum(jnp.stack([jnp.sum(a * b) for a, b in pairs]), ("gx", "gy"))
+    rz, zw, rz1, wz1, zw1, z1w1 = [dots[i] for i in range(6)]
+    first = rz / zw
+    next_rz = rz - first * (rz1 + zw) + first * first * wz1
+    grow = 1.0 + next_rz / rz
+    curve = grow * grow * zw - grow * first * (zw1 + wz1) + first * first * z1w1
+    second = next_rz / curve
+    c0 = first + second * grow
+    c1 = second * first
+    return (c0 * z0 - c1 * z1, right_side - c0 * w0 + c1 * w1)
 
 
 def solution(mesh):

time: 457 us -> 305 us (0.67)
  blocking collectives: 272 us -> 103 us
  starting transfers between devices: 84.6 us -> 100 us
  other arithmetic: 35.5 us -> 28 us
    psum x3 -> x1, blocking collectives: 272 us -> 103 us  [shards(): dots = lax.psum(jnp.stack([jnp.sum(a * b) for a, b in pairs]), ('gx', 'gy'))]
    ppermute x10, starting transfers between devices: 32.8 us -> 46.3 us  [with_halo(): lax.ppermute(lax.slice_in_dim(block, block.shape[dim] - width, None, axis...]
    ppermute x10, waiting for transfers between devices: 17.9 us -> 24.4 us  [with_halo(): lax.ppermute(lax.slice_in_dim(block, 0, width, axis=dim), axis, backward)]
  transfers between devices with their start and end apart: 28 -> 28, of which waited for: 13 -> 12; matrix products, arithmetic and copies ran while one was open for 1% -> 1% of each run, Pallas kernels for 0% -> 0%
where the time goes in v1:
time: 305 us; the launch traced here: 303 us
  blocking collectives  103 us (34%)
  starting transfers between devices  100 us (33%)
  waiting for transfers between devices  55.4 us (18%)
  other arithmetic  28 us (9%)
  between operations  8.22 us (3%)
  local copies, waits for them, and re-layouts  7.58 us (2%)
    psum x1, blocking collectives, shards(): dots = lax.psum(jnp.stack([jnp.sum(a * b) for a, b in pairs]), ('gx', 'gy'))  103 us
    ppermute x10, starting transfers between devices, with_halo(): lax.ppermute(lax.slice_in_dim(block, block.shape[dim] - width, None, axis...  46.3 us
    ppermute x8, starting transfers between devices, from_behind(): return lax.ppermute(x, axis, pairs)  37.1 us
    ppermute x8, waiting for transfers between devices, from_behind(): return lax.ppermute(x, axis, pairs)  27.7 us
    ppermute x10, waiting for transfers between devices, with_halo(): lax.ppermute(lax.slice_in_dim(block, 0, width, axis=dim), axis, backward)  24.4 us
    ppermute x10, starting transfers between devices, with_halo(): lax.ppermute(lax.slice_in_dim(block, 0, width, axis=dim), axis, backward)  17.1 us
    add x4, other arithmetic, chebyshev(): answer = answer + update  7.89 us
  transfers between devices with their start and end apart: 28, of which 12 were waited for; matrix products, arithmetic and copies ran while one was open for 1% of the time, Pallas kernels for 0%

profile of v1, /device:TPU:8, one launch (start us, length us, event | category | flops | bytes accessed | tf_op | source)
XLA Modules:
  0.0 303.1 jit_solution(976684894962176729)
XLA Ops:
  0.6 1.2 fusion.50
  1.8 1.8 collective-permute-start.4
  3.6 1.3 collective-permute-start.5
  6.0 1.3 collective-permute-start.1
  7.3 4.9 %collective-permute-start = (f32[5,128,128]{2,1,0:T(8,128)S(1)}, f32[5,128,128]{2,1,0:T(8,128)S(1)}, u32[]{:S(2)}, u32[]{:S(2)}) collective-permute-start(f32[5,128,128]{2,1,0:T(8,128)S(1)} %get-tuple-element.164), channel_id=1, source_target_pairs={{0,8},{8,16},{16,24},{24,32},{32,40},{40,48},{48,56},{56,64},{64,7... | collective-permute-start | bytes 983048 | tf_op jit(solution)/shard_map/ppermute | solution.py:21
  13.7 3.5 %collective-permute-start.2 = (f32[26,5,128]{2,1,0:T(8,128)S(1)}, f32[26,5,128]{2,1,0:T(8,128)S(1)}, u32[]{:S(2)}, u32[]{:S(2)}) collective-permute-start(f32[26,5,128]{2,1,0:T(8,128)S(1)} %get-tuple-element.139), channel_id=1, source_target_pairs={{0,1},{1,2},{2,3},{3,4},{4,5},{5,6},{6,7},{8,9},{9,10},{10,11},{11... | collective-permute-start | bytes 199688 | tf_op jit(solution)/shard_map/ppermute | solution.py:21
  17.2 2.4 collective-permute-start.3
  19.5 3.5 %collective-permute-start.6 = (f32[24,4,128]{2,1,0:T(4,128)S(1)}, f32[24,4,128]{2,1,0:T(4,128)S(1)}, u32[]{:S(2)}, u32[]{:S(2)}) collective-permute-start(f32[24,4,128]{2,1,0:T(4,128)S(1)} %get-tuple-element.147), channel_id=1, source_target_pairs={{0,1},{1,2},{2,3},{3,4},{4,5},{5,6},{6,7},{8,9},{9,10},{10,11},{11... | collective-permute-start | bytes 147464 | tf_op jit(solution)/shard_map/ppermute | solution.py:21
  23.0 2.4 collective-permute-start.7
  25.9 7.2 %collective-permute-done.7 = f32[24,4,128]{2,1,0:T(4,128)S(1)} collective-permute-done((f32[24,4,128]{2,1,0:T(4,128)S(1)}, f32[24,4,128]{2,1,0:T(4,128)S(1)}, u32[]{:S(2)}, u32[]{:S(2)}) %collective-permute-start.7) | collective-permute-done | bytes 49184 | tf_op jit(solution)/shard_map/ppermute | solution.py:24
  33.1 2.8 broadcast_multiply_fusion.1
  36.4 1.4 slice_multiply_fusion.13
  39.4 1.7 fusion.34
  42.1 1.7 add_add_fusion.1
  43.8 5.0 %collective-permute-start.8 = (f32[4,136,128]{2,1,0:T(8,128)S(1)}, f32[4,136,128]{2,1,0:T(8,128)S(1)}, u32[]{:S(2)}, u32[]{:S(2)}) collective-permute-start(f32[4,136,128]{2,1,0:T(8,128)S(1)} %get-tuple-element.144), channel_id=1, source_target_pairs={{0,8},{8,16},{16,24},{24,32},{32,40},{40,48},{48,56},{56,64},{64,7... | collective-permute-start | bytes 835592 | tf_op jit(solution)/shard_map/ppermute | solution.py:32
  48.8 1.3 collective-permute-start.9
  50.2 5.4 %collective-permute-done.9 = f32[4,136,128]{2,1,0:T(8,128)S(1)} collective-permute-done((f32[4,136,128]{2,1,0:T(8,128)S(1)}, f32[4,136,128]{2,1,0:T(8,128)S(1)}, u32[]{:S(2)}, u32[]{:S(2)}) %collective-permute-start.9) | collective-permute-done | bytes 278560 | tf_op jit(solution)/shard_map/ppermute | solution.py:32
  55.7 9.9 %collective-permute-start.10 = (f32[16,4,128]{2,1,0:T(4,128)S(1)}, f32[16,4,128]{2,1,0:T(4,128)S(1)}, u32[]{:S(2)}, u32[]{:S(2)}) collective-permute-start(f32[16,4,128]{2,1,0:T(4,128)S(1)} %get-tuple-element.156), channel_id=1, source_target_pairs={{0,1},{1,2},{2,3},{3,4},{4,5},{5,6},{6,7},{8,9},{9,10},{10,11},{11... | collective-permute-start | bytes 98312 | tf_op jit(solution)/shard_map/ppermute | solution.py:32
  65.8 1.9 collective-permute-start.11
  67.8 9.9 %collective-permute-done.11 = f32[16,4,128]{2,1,0:T(4,128)S(1)} collective-permute-done((f32[16,4,128]{2,1,0:T(4,128)S(1)}, f32[16,4,128]{2,1,0:T(4,128)S(1)}, u32[]{:S(2)}, u32[]{:S(2)}) %collective-permute-start.11) | collective-permute-done | bytes 32800 | tf_op jit(solution)/shard_map/ppermute | solution.py:32
  77.7 5.7 %collective-permute-start.13 = (f32[1,128,128]{2,1,0:T(8,128)S(1)}, f32[1,128,128]{2,1,0:T(8,128)S(1)}, u32[]{:S(2)}, u32[]{:S(2)}) collective-permute-start(f32[1,128,128]{2,1,0:T(8,128)S(1)} %get-tuple-element.161), channel_id=1, source_target_pairs={{0,8},{8,16},{16,24},{24,32},{32,40},{40,48},{48,56},{56,64},{64,7... | collective-permute-start | bytes 196616 | tf_op jit(solution)/shard_map/ppermute | solution.py:21
  83.4 1.3 collective-permute-start.12
  84.7 2.3 collective-permute-done.12
  87.1 1.9 collective-permute-start.14
  89.0 3.9 %collective-permute-start.15 = (f32[18,1,128]{2,1,0:T(1,128)S(1)}, f32[18,1,128]{2,1,0:T(1,128)S(1)}, u32[]{:S(2)}, u32[]{:S(2)}) collective-permute-start(f32[18,1,128]{2,1,0:T(1,128)S(1)} %get-tuple-element.152), channel_id=1, source_target_pairs={{0,1},{1,2},{2,3},{3,4},{4,5},{5,6},{6,7},{8,9},{9,10},{10,11},{11... | collective-permute-start | bytes 27656 | tf_op jit(solution)/shard_map/ppermute | solution.py:21
  95.7 3.7 %collective-permute-start.16 = (f32[4,128,128]{2,1,0:T(8,128)S(1)}, f32[4,128,128]{2,1,0:T(8,128)S(1)}, u32[]{:S(2)}, u32[]{:S(2)}) collective-permute-start(f32[4,128,128]{2,1,0:T(8,128)S(1)} %get-tuple-element.159), channel_id=1, source_target_pairs={{0,8},{8,16},{16,24},{24,32},{32,40},{40,48},{48,56},{56,64},{64,7... | collective-permute-start | bytes 786440 | tf_op jit(solution)/shard_map/ppermute | solution.py:21
  99.4 1.3 collective-permute-start.17
  100.7 2.7 collective-permute-done.17
  103.4 7.8 %collective-permute-start.18 = (f32[24,4,128]{2,1,0:T(4,128)S(1)}, f32[24,4,128]{2,1,0:T(4,128)S(1)}, u32[]{:S(2)}, u32[]{:S(2)}) collective-permute-start(f32[24,4,128]{2,1,0:T(4,128)S(1)} %get-tuple-element.145), channel_id=1, source_target_pairs={{0,1},{1,2},{2,3},{3,4},{4,5},{5,6},{6,7},{8,9},{9,10},{10,11},{11... | collective-permute-start | bytes 147464 | tf_op jit(solution)/shard_map/ppermute | solution.py:21
  111.2 2.1 collective-permute-start.19
  113.3 9.9 %collective-permute-done.19 = f32[24,4,128]{2,1,0:T(4,128)S(1)} collective-permute-done((f32[24,4,128]{2,1,0:T(4,128)S(1)}, f32[24,4,128]{2,1,0:T(4,128)S(1)}, u32[]{:S(2)}, u32[]{:S(2)}) %collective-permute-start.19) | collective-permute-done | bytes 49184 | tf_op jit(solution)/shard_map/ppermute | solution.py:24
  124.5 2.2 fusion.35
  128.1 2.3 add_add_fusion
  130.4 5.5 %collective-permute-start.20 = (f32[4,136,128]{2,1,0:T(8,128)S(1)}, f32[4,136,128]{2,1,0:T(8,128)S(1)}, u32[]{:S(2)}, u32[]{:S(2)}) collective-permute-start(f32[4,136,128]{2,1,0:T(8,128)S(1)} %get-tuple-element.142), channel_id=1, source_target_pairs={{0,8},{8,16},{16,24},{24,32},{32,40},{40,48},{48,56},{56,64},{64,7... | collective-permute-start | bytes 835592 | tf_op jit(solution)/shard_map/ppermute | solution.py:32
  135.9 1.3 collective-permute-start.21
  137.4 2.5 collective-permute-done.21
  140.0 10.2 %collective-permute-start.22 = (f32[16,4,128]{2,1,0:T(4,128)S(1)}, f32[16,4,128]{2,1,0:T(4,128)S(1)}, u32[]{:S(2)}, u32[]{:S(2)}) collective-permute-start(f32[16,4,128]{2,1,0:T(4,128)S(1)} %get-tuple-element.154), channel_id=1, source_target_pairs={{0,1},{1,2},{2,3},{3,4},{4,5},{5,6},{6,7},{8,9},{9,10},{10,11},{11... | collective-permute-start | bytes 98312 | tf_op jit(solution)/shard_map/ppermute | solution.py:32
  150.3 1.9 collective-permute-start.23
  152.2 9.9 %collective-permute-done.23 = f32[16,4,128]{2,1,0:T(4,128)S(1)} collective-permute-done((f32[16,4,128]{2,1,0:T(4,128)S(1)}, f32[16,4,128]{2,1,0:T(4,128)S(1)}, u32[]{:S(2)}, u32[]{:S(2)}) %collective-permute-start.23) | collective-permute-done | bytes 32800 | tf_op jit(solution)/shard_map/ppermute | solution.py:32
  162.2 7.6 %collective-permute-start.25 = (f32[1,128,128]{2,1,0:T(8,128)S(1)}, f32[1,128,128]{2,1,0:T(8,128)S(1)}, u32[]{:S(2)}, u32[]{:S(2)}) collective-permute-start(f32[1,128,128]{2,1,0:T(8,128)S(1)} %get-tuple-element.157), channel_id=1, source_target_pairs={{0,8},{8,16},{16,24},{24,32},{32,40},{40,48},{48,56},{56,64},{64,7... | collective-permute-start | bytes 196616 | tf_op jit(solution)/shard_map/ppermute | solution.py:21
  169.7 1.3 collective-permute-start.24
  171.1 2.3 collective-permute-done.24
  173.4 1.9 collective-permute-start.26
  175.3 3.9 %collective-permute-start.27 = (f32[18,1,128]{2,1,0:T(1,128)S(1)}, f32[18,1,128]{2,1,0:T(1,128)S(1)}, u32[]{:S(2)}, u32[]{:S(2)}) collective-permute-start(f32[18,1,128]{2,1,0:T(1,128)S(1)} %get-tuple-element.150), channel_id=1, source_target_pairs={{0,1},{1,2},{2,3},{3,4},{4,5},{5,6},{6,7},{8,9},{9,10},{10,11},{11... | collective-permute-start | bytes 27656 | tf_op jit(solution)/shard_map/ppermute | solution.py:21
  180.9 4.1 %multiply_reduce_fusion = (f32[]{:T(128)}, f32[]{:T(128)}, f32[]{:T(128)}, f32[]{:T(128)}, f32[]{:T(128)}, /*index=5*/f32[]{:T(128)}, f32[16,128,128]{2,1,0:T(8,128)}) fusion(f32[16,128,128]{2,1,0:T(8,128)S(1)} %fusion.30, f32[16,128,128]{2,1,0:T(8,128)S(1)} %fusion.32, f32[16,128,128]{2,1,0:T(8,128)S(1)} %fusion.20, f32[16,128,128]{2,1,0:T(8,128)S(1)} %copy-done, ...), kind=kLoop, calls=%fused_computation.89 | loop fusion | flops 8126458 | bytes 12716056 | tf_op jit(solution)/shard_map/reduce_sum | solution.py:146
  185.0 3.8 %stack.27 = f32[6]{0:T(128)S(1)} concatenate(f32[1]{0:T(128)} %bitcast, f32[1]{0:T(128)} %bitcast.1, f32[1]{0:T(128)} %bitcast.2, f32[1]{0:T(128)} %bitcast.3, f32[1]{0:T(128)} %bitcast.4, f32[1]{0:T(128)} %bitcast.5), dimensions={0} | concatenate | bytes 48 | tf_op jit(solution)/shard_map/stack | solution.py:146
  188.8 103.4 %psum.7 = f32[6]{0:T(128)S(1)} all-reduce(f32[6]{0:T(128)S(1)} %stack.27), channel_id=1, replica_groups=mesh['gx'=32,'gy'=8] {'gx','gy'}, use_global_device_ids=true, to_apply=%region_6.7 | all-reduce | flops 6 | bytes 48 | tf_op jit(solution)/shard_map/psum | solution.py:146
  299.7 3.3 %multiply_add_fusion.2 = (f32[16,128,128]{2,1,0:T(8,128)}, f32[16,128,128]{2,1,0:T(8,128)}) fusion(f32[16,128,128]{2,1,0:T(8,128)} %get-tuple-element.104, f32[16,128,128]{2,1,0:T(8,128)} %param.18, f32[16,128,128]{2,1,0:T(8,128)S(1)} %fusion.20, f32[]{:T(128)S(6)} %mul.355, f32[]{:T(128)S(6)} %add.362, f32[16,128,128]{2,1,0:T(8,128)S(1)} %fusion.30, ...), kind=kLoop, calls=%fused_computation.87 | loop fusion | flops 1835008 | bytes 7340040 | tf_op jit(solution)/shard_map/add | solution.py:155
  (75 shorter events, 14.4 us)
Async XLA Ops:
  0.6 11.6 %copy-start = (f32[16,128,128]{2,1,0:T(8,128)S(1)}, f32[16,128,128]{2,1,0:T(8,128)}, u32[]{:S(2)}) copy-start(f32[16,128,128]{2,1,0:T(8,128)} %param.18) | copy-start | bytes 3145732
  1.8 10.4 %collective-permute-start.4 = (f32[4,128,128]{2,1,0:T(8,128)S(1)}, f32[4,128,128]{2,1,0:T(8,128)S(1)}, u32[]{:S(2)}, u32[]{:S(2)}) collective-permute-start(f32[4,128,128]{2,1,0:T(8,128)S(1)} %get-tuple-element.166), channel_id=1, source_target_pairs={{0,8},{8,16},{16,24},{24,32},{32,40},{40,48},{48,56},{56,64},{64,7... | collective-permute-start | bytes 786440 | tf_op jit(solution)/shard_map/ppermute | solution.py:21
  3.6 8.8 %collective-permute-start.5 = (f32[4,128,128]{2,1,0:T(8,128)S(1)}, f32[4,128,128]{2,1,0:T(8,128)S(1)}, u32[]{:S(2)}, u32[]{:S(2)}) collective-permute-start(f32[4,128,128]{2,1,0:T(8,128)S(1)} %get-tuple-element.165), channel_id=1, source_target_pairs={{8,0},{16,8},{24,16},{32,24},{40,32},{48,40},{56,48},{64,56},{72,6... | collective-permute-start | bytes 786440 | tf_op jit(solution)/shard_map/ppermute | solution.py:24
  6.0 7.6 %collective-permute-start.1 = (f32[5,128,128]{2,1,0:T(8,128)S(1)}, f32[5,128,128]{2,1,0:T(8,128)S(1)}, u32[]{:S(2)}, u32[]{:S(2)}) collective-permute-start(f32[5,128,128]{2,1,0:T(8,128)S(1)} %get-tuple-element.163), channel_id=1, source_target_pairs={{8,0},{16,8},{24,16},{32,24},{40,32},{48,40},{56,48},{64,56},{72,6... | collective-permute-start | bytes 983048 | tf_op jit(solution)/shard_map/ppermute | solution.py:24
  7.3 6.2 %collective-permute-start = (f32[5,128,128]{2,1,0:T(8,128)S(1)}, f32[5,128,128]{2,1,0:T(8,128)S(1)}, u32[]{:S(2)}, u32[]{:S(2)}) collective-permute-start(f32[5,128,128]{2,1,0:T(8,128)S(1)} %get-tuple-element.164), channel_id=1, source_target_pairs={{0,8},{8,16},{16,24},{24,32},{32,40},{40,48},{48,56},{56,64},{64,7... | collective-permute-start | bytes 983048 | tf_op jit(solution)/shard_map/ppermute | solution.py:21
  12.3 1.2 copy-start.1
  13.7 11.7 %collective-permute-start.2 = (f32[26,5,128]{2,1,0:T(8,128)S(1)}, f32[26,5,128]{2,1,0:T(8,128)S(1)}, u32[]{:S(2)}, u32[]{:S(2)}) collective-permute-start(f32[26,5,128]{2,1,0:T(8,128)S(1)} %get-tuple-element.139), channel_id=1, source_target_pairs={{0,1},{1,2},{2,3},{3,4},{4,5},{5,6},{6,7},{8,9},{9,10},{10,11},{11... | collective-permute-start | bytes 199688 | tf_op jit(solution)/shard_map/ppermute | solution.py:21
  17.2 8.3 %collective-permute-start.3 = (f32[26,5,128]{2,1,0:T(8,128)S(1)}, f32[26,5,128]{2,1,0:T(8,128)S(1)}, u32[]{:S(2)}, u32[]{:S(2)}) collective-permute-start(f32[26,5,128]{2,1,0:T(8,128)S(1)} %get-tuple-element.140), channel_id=1, source_target_pairs={{1,0},{2,1},{3,2},{4,3},{5,4},{6,5},{7,6},{9,8},{10,9},{11,10},{12... | collective-permute-start | bytes 199688 | tf_op jit(solution)/shard_map/ppermute | solution.py:24
  19.5 6.4 %collective-permute-start.6 = (f32[24,4,128]{2,1,0:T(4,128)S(1)}, f32[24,4,128]{2,1,0:T(4,128)S(1)}, u32[]{:S(2)}, u32[]{:S(2)}) collective-permute-start(f32[24,4,128]{2,1,0:T(4,128)S(1)} %get-tuple-element.147), channel_id=1, source_target_pairs={{0,1},{1,2},{2,3},{3,4},{4,5},{5,6},{6,7},{8,9},{9,10},{10,11},{11... | collective-permute-start | bytes 147464 | tf_op jit(solution)/shard_map/ppermute | solution.py:21
  23.0 10.1 %collective-permute-start.7 = (f32[24,4,128]{2,1,0:T(4,128)S(1)}, f32[24,4,128]{2,1,0:T(4,128)S(1)}, u32[]{:S(2)}, u32[]{:S(2)}) collective-permute-start(f32[24,4,128]{2,1,0:T(4,128)S(1)} %get-tuple-element.148), channel_id=1, source_target_pairs={{1,0},{2,1},{3,2},{4,3},{5,4},{6,5},{7,6},{9,8},{10,9},{11,10},{12... | collective-permute-start | bytes 147464 | tf_op jit(solution)/shard_map/ppermute | solution.py:24
  43.8 6.4 %collective-permute-start.8 = (f32[4,136,128]{2,1,0:T(8,128)S(1)}, f32[4,136,128]{2,1,0:T(8,128)S(1)}, u32[]{:S(2)}, u32[]{:S(2)}) collective-permute-start(f32[4,136,128]{2,1,0:T(8,128)S(1)} %get-tuple-element.144), channel_id=1, source_target_pairs={{0,8},{8,16},{16,24},{24,32},{32,40},{40,48},{48,56},{56,64},{64,7... | collective-permute-start | bytes 835592 | tf_op jit(solution)/shard_map/ppermute | solution.py:32
  48.8 6.9 %collective-permute-start.9 = (f32[4,136,128]{2,1,0:T(8,128)S(1)}, f32[4,136,128]{2,1,0:T(8,128)S(1)}, u32[]{:S(2)}, u32[]{:S(2)}) collective-permute-start(f32[4,136,128]{2,1,0:T(8,128)S(1)} %get-tuple-element.143), channel_id=1, source_target_pairs={{8,0},{16,8},{24,16},{32,24},{40,32},{48,40},{56,48},{64,56},{72,6... | collective-permute-start | bytes 835592 | tf_op jit(solution)/shard_map/ppermute | solution.py:32
  55.7 12.0 %collective-permute-start.10 = (f32[16,4,128]{2,1,0:T(4,128)S(1)}, f32[16,4,128]{2,1,0:T(4,128)S(1)}, u32[]{:S(2)}, u32[]{:S(2)}) collective-permute-start(f32[16,4,128]{2,1,0:T(4,128)S(1)} %get-tuple-element.156), channel_id=1, source_target_pairs={{0,1},{1,2},{2,3},{3,4},{4,5},{5,6},{6,7},{8,9},{9,10},{10,11},{11... | collective-permute-start | bytes 98312 | tf_op jit(solution)/shard_map/ppermute | solution.py:32
  65.8 11.9 %collective-permute-start.11 = (f32[16,4,128]{2,1,0:T(4,128)S(1)}, f32[16,4,128]{2,1,0:T(4,128)S(1)}, u32[]{:S(2)}, u32[]{:S(2)}) collective-permute-start(f32[16,4,128]{2,1,0:T(4,128)S(1)} %get-tuple-element.155), channel_id=1, source_target_pairs={{1,0},{2,1},{3,2},{4,3},{5,4},{6,5},{7,6},{9,8},{10,9},{11,10},{12... | collective-permute-start | bytes 98312 | tf_op jit(solution)/shard_map/ppermute | solution.py:32
  77.7 7.0 %collective-permute-start.13 = (f32[1,128,128]{2,1,0:T(8,128)S(1)}, f32[1,128,128]{2,1,0:T(8,128)S(1)}, u32[]{:S(2)}, u32[]{:S(2)}) collective-permute-start(f32[1,128,128]{2,1,0:T(8,128)S(1)} %get-tuple-element.161), channel_id=1, source_target_pairs={{0,8},{8,16},{16,24},{24,32},{32,40},{40,48},{48,56},{56,64},{64,7... | collective-permute-start | bytes 196616 | tf_op jit(solution)/shard_map/ppermute | solution.py:21
  83.4 3.6 %collective-permute-start.12 = (f32[1,128,128]{2,1,0:T(8,128)S(1)}, f32[1,128,128]{2,1,0:T(8,128)S(1)}, u32[]{:S(2)}, u32[]{:S(2)}) collective-permute-start(f32[1,128,128]{2,1,0:T(8,128)S(1)} %get-tuple-element.162), channel_id=1, source_target_pairs={{8,0},{16,8},{24,16},{32,24},{40,32},{48,40},{56,48},{64,56},{72,6... | collective-permute-start | bytes 196616 | tf_op jit(solution)/shard_map/ppermute | solution.py:24
  87.1 6.3 %collective-permute-start.14 = (f32[18,1,128]{2,1,0:T(1,128)S(1)}, f32[18,1,128]{2,1,0:T(1,128)S(1)}, u32[]{:S(2)}, u32[]{:S(2)}) collective-permute-start(f32[18,1,128]{2,1,0:T(1,128)S(1)} %get-tuple-element.151), channel_id=1, source_target_pairs={{1,0},{2,1},{3,2},{4,3},{5,4},{6,5},{7,6},{9,8},{10,9},{11,10},{12... | collective-permute-start | bytes 27656 | tf_op jit(solution)/shard_map/ppermute | solution.py:24
  89.0 5.6 %collective-permute-start.15 = (f32[18,1,128]{2,1,0:T(1,128)S(1)}, f32[18,1,128]{2,1,0:T(1,128)S(1)}, u32[]{:S(2)}, u32[]{:S(2)}) collective-permute-start(f32[18,1,128]{2,1,0:T(1,128)S(1)} %get-tuple-element.152), channel_id=1, source_target_pairs={{0,1},{1,2},{2,3},{3,4},{4,5},{5,6},{6,7},{8,9},{9,10},{10,11},{11... | collective-permute-start | bytes 27656 | tf_op jit(solution)/shard_map/ppermute | solution.py:21
  95.7 5.0 %collective-permute-start.16 = (f32[4,128,128]{2,1,0:T(8,128)S(1)}, f32[4,128,128]{2,1,0:T(8,128)S(1)}, u32[]{:S(2)}, u32[]{:S(2)}) collective-permute-start(f32[4,128,128]{2,1,0:T(8,128)S(1)} %get-tuple-element.159), channel_id=1, source_target_pairs={{0,8},{8,16},{16,24},{24,32},{32,40},{40,48},{48,56},{56,64},{64,7... | collective-permute-start | bytes 786440 | tf_op jit(solution)/shard_map/ppermute | solution.py:21
  99.4 4.0 %collective-permute-start.17 = (f32[4,128,128]{2,1,0:T(8,128)S(1)}, f32[4,128,128]{2,1,0:T(8,128)S(1)}, u32[]{:S(2)}, u32[]{:S(2)}) collective-permute-start(f32[4,128,128]{2,1,0:T(8,128)S(1)} %get-tuple-element.160), channel_id=1, source_target_pairs={{8,0},{16,8},{24,16},{32,24},{40,32},{48,40},{56,48},{64,56},{72,6... | collective-permute-start | bytes 786440 | tf_op jit(solution)/shard_map/ppermute | solution.py:24
  103.4 9.9 %collective-permute-start.18 = (f32[24,4,128]{2,1,0:T(4,128)S(1)}, f32[24,4,128]{2,1,0:T(4,128)S(1)}, u32[]{:S(2)}, u32[]{:S(2)}) collective-permute-start(f32[24,4,128]{2,1,0:T(4,128)S(1)} %get-tuple-element.145), channel_id=1, source_target_pairs={{0,1},{1,2},{2,3},{3,4},{4,5},{5,6},{6,7},{8,9},{9,10},{10,11},{11... | collective-permute-start | bytes 147464 | tf_op jit(solution)/shard_map/ppermute | solution.py:21
  111.2 12.0 %collective-permute-start.19 = (f32[24,4,128]{2,1,0:T(4,128)S(1)}, f32[24,4,128]{2,1,0:T(4,128)S(1)}, u32[]{:S(2)}, u32[]{:S(2)}) collective-permute-start(f32[24,4,128]{2,1,0:T(4,128)S(1)} %get-tuple-element.146), channel_id=1, source_target_pairs={{1,0},{2,1},{3,2},{4,3},{5,4},{6,5},{7,6},{9,8},{10,9},{11,10},{12... | collective-permute-start | bytes 147464 | tf_op jit(solution)/shard_map/ppermute | solution.py:24
  130.4 6.9 %collective-permute-start.20 = (f32[4,136,128]{2,1,0:T(8,128)S(1)}, f32[4,136,128]{2,1,0:T(8,128)S(1)}, u32[]{:S(2)}, u32[]{:S(2)}) collective-permute-start(f32[4,136,128]{2,1,0:T(8,128)S(1)} %get-tuple-element.142), channel_id=1, source_target_pairs={{0,8},{8,16},{16,24},{24,32},{32,40},{40,48},{48,56},{56,64},{64,7... | collective-permute-start | bytes 835592 | tf_op jit(solution)/shard_map/ppermute | solution.py:32
  135.9 3.9 %collective-permute-start.21 = (f32[4,136,128]{2,1,0:T(8,128)S(1)}, f32[4,136,128]{2,1,0:T(8,128)S(1)}, u32[]{:S(2)}, u32[]{:S(2)}) collective-permute-start(f32[4,136,128]{2,1,0:T(8,128)S(1)} %get-tuple-element.141), channel_id=1, source_target_pairs={{8,0},{16,8},{24,16},{32,24},{40,32},{48,40},{56,48},{64,56},{72,6... | collective-permute-start | bytes 835592 | tf_op jit(solution)/shard_map/ppermute | solution.py:32
  140.0 12.3 %collective-permute-start.22 = (f32[16,4,128]{2,1,0:T(4,128)S(1)}, f32[16,4,128]{2,1,0:T(4,128)S(1)}, u32[]{:S(2)}, u32[]{:S(2)}) collective-permute-start(f32[16,4,128]{2,1,0:T(4,128)S(1)} %get-tuple-element.154), channel_id=1, source_target_pairs={{0,1},{1,2},{2,3},{3,4},{4,5},{5,6},{6,7},{8,9},{9,10},{10,11},{11... | collective-permute-start | bytes 98312 | tf_op jit(solution)/shard_map/ppermute | solution.py:32
  150.3 11.8 %collective-permute-start.23 = (f32[16,4,128]{2,1,0:T(4,128)S(1)}, f32[16,4,128]{2,1,0:T(4,128)S(1)}, u32[]{:S(2)}, u32[]{:S(2)}) collective-permute-start(f32[16,4,128]{2,1,0:T(4,128)S(1)} %get-tuple-element.153), channel_id=1, source_target_pairs={{1,0},{2,1},{3,2},{4,3},{5,4},{6,5},{7,6},{9,8},{10,9},{11,10},{12... | collective-permute-start | bytes 98312 | tf_op jit(solution)/shard_map/ppermute | solution.py:32
  162.2 8.9 %collective-permute-start.25 = (f32[1,128,128]{2,1,0:T(8,128)S(1)}, f32[1,128,128]{2,1,0:T(8,128)S(1)}, u32[]{:S(2)}, u32[]{:S(2)}) collective-permute-start(f32[1,128,128]{2,1,0:T(8,128)S(1)} %get-tuple-element.157), channel_id=1, source_target_pairs={{0,8},{8,16},{16,24},{24,32},{32,40},{40,48},{48,56},{56,64},{64,7... | collective-permute-start | bytes 196616 | tf_op jit(solution)/shard_map/ppermute | solution.py:21
  169.7 3.6 %collective-permute-start.24 = (f32[1,128,128]{2,1,0:T(8,128)S(1)}, f32[1,128,128]{2,1,0:T(8,128)S(1)}, u32[]{:S(2)}, u32[]{:S(2)}) collective-permute-start(f32[1,128,128]{2,1,0:T(8,128)S(1)} %get-tuple-element.158), channel_id=1, source_target_pairs={{8,0},{16,8},{24,16},{32,24},{40,32},{48,40},{56,48},{64,56},{72,6... | collective-permute-start | bytes 196616 | tf_op jit(solution)/shard_map/ppermute | solution.py:24
  173.4 6.4 %collective-permute-start.26 = (f32[18,1,128]{2,1,0:T(1,128)S(1)}, f32[18,1,128]{2,1,0:T(1,128)S(1)}, u32[]{:S(2)}, u32[]{:S(2)}) collective-permute-start(f32[18,1,128]{2,1,0:T(1,128)S(1)} %get-tuple-element.149), channel_id=1, source_target_pairs={{1,0},{2,1},{3,2},{4,3},{5,4},{6,5},{7,6},{9,8},{10,9},{11,10},{12... | collective-permute-start | bytes 27656 | tf_op jit(solution)/shard_map/ppermute | solution.py:24
  175.3 5.6 %collective-permute-start.27 = (f32[18,1,128]{2,1,0:T(1,128)S(1)}, f32[18,1,128]{2,1,0:T(1,128)S(1)}, u32[]{:S(2)}, u32[]{:S(2)}) collective-permute-start(f32[18,1,128]{2,1,0:T(1,128)S(1)} %get-tuple-element.150), channel_id=1, source_target_pairs={{0,1},{1,2},{2,3},{3,4},{4,5},{5,6},{6,7},{8,9},{9,10},{10,11},{11... | collective-permute-start | bytes 27656 | tf_op jit(solution)/shard_map/ppermute | solution.py:21

commit v2 on v1

v2 whole, which is shorter than its diff:
```python
import itertools

import jax
import jax.numpy as jnp
from jax import lax
from jax.experimental import pallas as pl
from jax.experimental.pallas import tpu as pltpu
from jax.sharding import PartitionSpec as P

MESH = pl.DeviceIdType.MESH
MARGIN = 4
absorb = 0.05
theta = 1.05
delta = 0.95

sig = theta / delta
rho0 = 1.0 / sig
rho1 = 1.0 / (2.0 * sig - rho0)
rho2 = 1.0 / (2.0 * sig - rho1)
c1, c2 = rho1 * rho0, 2.0 * rho1 / delta
c3, c4 = rho2 * rho1, 2.0 * rho2 / delta
A1 = 1.0 + c1 + c2 * (theta - 1.0)
B1 = 0.5 * c2
A2 = 1.0 + c3 - c4
A0 = c4 * theta - c3
B2 = 0.5 * c4

KW, RW = 7, 6
GUARD = 8
YO = 16
XO = KW

SIZES = dict(c=2, x=4, z=4, y=4, h=2)
STAGES = (("c",), ("x", "y"), ("z", "h"))
NEAR = tuple((dx, dy) for dx in (-1, 0, 1) for dy in (-1, 0, 1) if (dx, dy) != (0, 0))


def offsets(dims):
    return [o for o in itertools.product(*[range(SIZES[d]) for d in dims]) if any(o)]


N_SLOTS = sum(len(offsets(dims)) for dims in STAGES)


def partner(gx, gy, dims, off):
    me = dict(c=gx % 2, x=(gx // 2) % 4, z=gx // 8, y=gy % 4, h=gy // 4)
    for d, o in zip(dims, off):
        me[d] = (me[d] + o) % SIZES[d]
    return (me["z"] * 8 + me["x"] * 2 + me["c"], me["h"] * 4 + me["y"])


def kernel(
    r_hbm, k_hbm, sol_hbm, res_hbm,
    K, R, INV, DIAG, FX, FY, FZ, Y0, Y1, Y0B, Z0, Z1, W0, W1, part, slots,
    load_sem, out_sem, send_sem, recv_sem, ar_send, ar_recv,
):
    cx, cy, nz = r_hbm.shape
    n_gx, n_gy = lax.axis_size("gx"), lax.axis_size("gy")
    gx, gy = lax.axis_index("gx"), lax.axis_index("gy")
    n_tiles = cy // 8

    def here(dx, dy):
        return (gx + dx >= 0) & (gx + dx < n_gx) & (gy + dy >= 0) & (gy + dy < n_gy)

    barrier = pltpu.get_barrier_semaphore()
    count = 0
    for dx, dy in NEAR:
        count = count + here(dx, dy).astype(jnp.int32)

        @pl.when(here(dx, dy))
        def _():
            pl.semaphore_signal(barrier, inc=1, device_id=(gx + dx, gy + dy), device_id_type=MESH)

    for dims in STAGES:
        for off in offsets(dims):
            pl.semaphore_signal(
                barrier, inc=1, device_id=partner(gx, gy, dims, off), device_id_type=MESH
            )
            count = count + 1

    own = (pl.ds(XO, cx), pl.ds(YO, cy))
    loads = [
        pltpu.make_async_copy(k_hbm, K.at[own], load_sem.at[0]),
        pltpu.make_async_copy(r_hbm, R.at[own], load_sem.at[1]),
    ]
    for load in loads:
        load.start()
    pl.semaphore_wait(barrier, count)

    def halo_copies(k, dx, dy):
        out = []
        for n, (src, dst, width) in enumerate(((k_hbm, K, KW), (r_hbm, R, RW))):
            if dx > 0:
                sx, tx = pl.ds(cx - width, width), pl.ds(XO - width, width)
            elif dx < 0:
                sx, tx = pl.ds(0, width), pl.ds(XO + cx, width)
            else:
                sx, tx = pl.ds(0, cx), pl.ds(XO, cx)
            if dy > 0:
                sy, ty = pl.ds(cy - 8, 8), pl.ds(YO - 8, 8)
            elif dy < 0:
                sy, ty = pl.ds(0, 8), pl.ds(YO + cy, 8)
            else:
                sy, ty = pl.ds(0, cy), pl.ds(YO, cy)
            out.append(
                pltpu.make_async_remote_copy(
                    src.at[sx, sy], dst.at[tx, ty], send_sem.at[2 * k + n], recv_sem.at[2 * k + n],
                    device_id=(gx + dx, gy + dy), device_id_type=MESH,
                )
            )
        return out

    for k, (dx, dy) in enumerate(NEAR):

        @pl.when(here(dx, dy))
        def _():
            for copy in halo_copies(k, dx, dy):
                copy.start()

    rows = cy + 16
    flat = lambda n: jnp.zeros((n, nz), jnp.float32)

    @pl.when(gx == 0)
    def _():
        for x in range(XO):
            K[x, pl.ds(YO - 8, rows)] = flat(rows)
            R[x, pl.ds(YO - 8, rows)] = flat(rows)

    @pl.when(gx == n_gx - 1)
    def _():
        for x in range(XO + cx, XO + cx + KW):
            K[x, pl.ds(YO - 8, rows)] = flat(rows)
            R[x, pl.ds(YO - 8, rows)] = flat(rows)

    for load in loads:
        load.wait()
    for k, (dx, dy) in enumerate(NEAR):

        @pl.when(here(-dx, -dy))
        def _():
            for copy in halo_copies(k, dx, dy):
                copy.wait_recv()

    @pl.when(gx == 0)
    def _():
        K[XO - 1, pl.ds(YO - 8, rows)] = K[XO, pl.ds(YO - 8, rows)]

    @pl.when(gx == n_gx - 1)
    def _():
        K[XO + cx, pl.ds(YO - 8, rows)] = K[XO + cx - 1, pl.ds(YO - 8, rows)]

    n_layers = cx + 2 * KW

    @pl.when(gy == 0)
    def _():
        for x in range(n_layers):
            K[x, pl.ds(YO - 8, 8)] = jnp.broadcast_to(K[x, pl.ds(YO, 1)], (8, nz))
            R[x, pl.ds(YO - 8, 8)] = flat(8)

    @pl.when(gy == n_gy - 1)
    def _():
        for x in range(n_layers):
            K[x, pl.ds(YO + cy, 8)] = jnp.broadcast_to(K[x, pl.ds(YO + cy - 1, 1)], (8, nz))
            R[x, pl.ds(YO + cy, 8)] = flat(8)

    lane = lax.broadcasted_iota(jnp.int32, (8, nz), 1)
    sub = lax.broadcasted_iota(jnp.int32, (8, nz), 0)
    first_lane, last_lane = lane == 0, lane == nz - 1
    one = jnp.float32(1.0)
    m_lo = jnp.where(gx > 0, one, 0.0)
    m_hi = jnp.where(gx < n_gx - 1, one, 0.0)
    has_lo, has_hi = gy > 0, gy < n_gy - 1
    n_lo = jnp.where(has_lo, one, 0.0)
    n_hi = jnp.where(has_hi, one, 0.0)

    def at(ref, x, row):
        return ref[x + XO, pl.ds(row, 8), :]

    def put(ref, x, row, value):
        ref[x + XO, pl.ds(row, 8), :] = value

    def tile_row(t):
        return pl.multiple_of(YO - 8 + 8 * t, 8)

    def coefficients(t, carry):
        r0 = tile_row(t)
        low, mid = at(K, -RW - 1, r0), at(K, -RW, r0)
        for x in range(-RW, cx + RW):
            high = at(K, x + 1, r0)
            up, down = at(K, x, r0 + 1), at(K, x, r0 - 1)
            right = jnp.where(last_lane, mid, pltpu.roll(mid, nz - 1, 1))
            left = jnp.where(first_lane, mid, pltpu.roll(mid, 1, 1))
            diag = (absorb + 3.0 * mid) + 0.5 * ((low + high) + (up + down) + (left + right))
            inv = 1.0 / diag
            put(DIAG, x, r0, diag)
            put(INV, x, r0, inv)
            put(FX, x, r0, mid + high)
            put(FY, x, r0, mid + up)
            put(FZ, x, r0, jnp.where(last_lane, 0.0, mid + right))
            put(Y0, x, r0, at(R, x, r0) * (inv * (1.0 / theta)))
            low, mid = mid, high
        return carry

    lax.fori_loop(0, n_tiles + 2, coefficients, 0)

    @pl.when(gx == 0)
    def _():
        FX[XO - 1, pl.ds(YO - 8, rows)] = flat(rows)

    @pl.when(gx == n_gx - 1)
    def _():
        FX[XO + cx - 1, pl.ds(YO - 8, rows)] = flat(rows)

    @pl.when(gy == 0)
    def _():
        for x in range(n_layers):
            FY[x, pl.ds(YO - 1, 1)] = flat(1)

    @pl.when(gy == n_gy - 1)
    def _():
        for x in range(n_layers):
            FY[x, pl.ds(YO + cy - 1, 1)] = flat(1)

    def sweep(src, lo, hi, r0, use):
        prev, cur, f_prev = at(src, lo - 1, r0), at(src, lo, r0), at(FX, lo - 1, r0)
        for x in range(lo, hi):
            nxt, f = at(src, x + 1, r0), at(FX, x, r0)
            fz = at(FZ, x, r0)
            total = f * nxt + f_prev * prev
            total = total + (at(FY, x, r0) * at(src, x, r0 + 1) + at(FY, x, r0 - 1) * at(src, x, r0 - 1))
            total = total + (fz * pltpu.roll(cur, nz - 1, 1) + pltpu.roll(fz * cur, 1, 1))
            use(x, cur, total)
            prev, cur, f_prev = cur, nxt, f

    def in_overlap(row):
        return ((row >= -MARGIN) & (row < MARGIN) & has_lo) | (
            (row >= cy - MARGIN) & (row < cy + MARGIN) & has_hi
        )

    def precondition(y0, y1, z, reach):
        def first(t, carry):
            r0 = tile_row(t)

            def use(x, value, total):
                put(y1, x, r0, A1 * value + B1 * (at(INV, x, r0) * total))

            sweep(y0, -reach - 1, cx + reach + 1, r0, use)
            return carry

        lax.fori_loop(0, n_tiles + 2, first, 0)

        edges = [(MARGIN - 1, 1, m_lo), (cx - MARGIN, -1, m_hi)]
        if reach == MARGIN:
            edges += [(-MARGIN, -1, one), (cx + MARGIN - 1, 1, one)]

        def second(t, carry):
            r0 = tile_row(t)
            row = sub + (r0 - YO)
            over = jnp.where(in_overlap(row), one, 0.0)
            pair_up = 1.0 + over * jnp.where(in_overlap(row + 1), one, 0.0)
            pair_down = 1.0 + over * jnp.where(in_overlap(row - 1), one, 0.0)
            times = 1.0 + over
            t_lo, t_hi = times * (1.0 + m_lo), times * (1.0 + m_hi)
            fixes = {}

            def cut(x, value):
                fixes[x] = value if x not in fixes else fixes[x] + value

            for a, d, weight in edges:
                def face(row0):
                    return at(FX, a if d > 0 else a - 1, row0)

                def e_at(row0):
                    return B1 * (at(INV, a, row0) * (face(row0) * at(y0, a + d, row0)))

                e, e_up, e_down = e_at(r0), e_at(r0 + 1), e_at(r0 - 1)
                fz, inv = at(FZ, a, r0), at(INV, a, r0)
                flow = face(r0) * at(y1, a + d, r0) + (
                    fz * pltpu.roll(e, nz - 1, 1) + pltpu.roll(fz * e, 1, 1)
                )
                side = at(FY, a, r0) * (pair_up * e_up) + at(FY, a, r0 - 1) * (pair_down * e_down)
                cut(a, weight * (times * (A2 * e + B2 * (inv * flow)) + B2 * (inv * side)))
                inner = at(FX, a - 1 if d > 0 else a, r0)
                cut(a - d, (weight * B2) * (times * (at(INV, a - d, r0) * (inner * e))))

            def use(x, value, total):
                y2 = A2 * value + A0 * at(y0, x, r0) + B2 * (at(INV, x, r0) * total)
                scale = t_lo if x < MARGIN else (t_hi if x >= cx - MARGIN else times)
                out = scale * y2
                if x in fixes:
                    out = out - fixes[x]
                put(z, x, r0, out)

            sweep(y1, -reach, cx + reach, r0, use)
            return carry

        lax.fori_loop(0, n_tiles + 2, second, 0)

        def over_x(x):
            if -MARGIN <= x < MARGIN:
                return m_lo
            if cx - MARGIN <= x < cx + MARGIN:
                return m_hi
            return 0.0

        def up(v):
            return pltpu.roll(v, 7, 0)

        def down(v):
            return pltpu.roll(v, 1, 0)

        sides = [(YO, 1, n_lo), (YO + cy - 8, -1, n_hi)]
        if reach == MARGIN:
            sides += [(YO - 8, -1, one), (YO + cy, 1, one)]
        for r0, d, weight in sides:
            edge = sub == (3 if d > 0 else 4)
            inner = sub == (2 if d > 0 else 5)

            def cross(fy, v):
                return fy * up(v) if d > 0 else down(fy * v)

            def e_of(x):
                return jnp.where(edge, B1 * (at(INV, x, r0) * cross(at(FY, x, r0), at(y0, x, r0))), 0.0)

            prev, cur, f_prev = e_of(-reach - 1), e_of(-reach), at(FX, -reach - 1, r0)
            for x in range(-reach, cx + reach):
                nxt, f = e_of(x + 1), at(FX, x, r0)
                fy, fz, inv = at(FY, x, r0), at(FZ, x, r0), at(INV, x, r0)
                times = 1.0 + over_x(x)
                flow = jnp.where(edge, cross(fy, at(y1, x, r0)), 0.0)
                flow = flow + jnp.where(inner, cross(fy, cur), 0.0)
                flow = flow + (fz * pltpu.roll(cur, nz - 1, 1) + pltpu.roll(fz * cur, 1, 1))
                side = (1.0 + over_x(x) * over_x(x + 1)) * (f * nxt) if x + 1 != MARGIN and x + 1 != cx - MARGIN else f * nxt
                side = side + (
                    (1.0 + over_x(x) * over_x(x - 1)) * (f_prev * prev)
                    if x != MARGIN and x != cx - MARGIN else f_prev * prev
                )
                fix = times * (A2 * cur + B2 * (inv * flow)) + B2 * (inv * side)
                put(z, x, r0, at(z, x, r0) - weight * fix)
                prev, cur, f_prev = cur, nxt, f

    zero = jnp.zeros((8, nz), jnp.float32)
    precondition(Y0, Y1, Z0, MARGIN)

    def own_row(t):
        return pl.multiple_of(YO + 8 * t, 8)

    def image0(r0, inside, carry):
        rz, zw = carry

        def use(x, value, total):
            nonlocal rz, zw
            half = 0.5 * total
            put(Y0B, x, r0, (value - at(INV, x, r0) * half) * (1.0 / theta))
            if inside and 0 <= x < cx:
                w = at(DIAG, x, r0) * value - half
                put(W0, x - XO, r0 - YO, w)
                rz = rz + at(R, x, r0) * value
                zw = zw + value * w

        sweep(Z0, -3, cx + 3, r0, use)
        return rz, zw

    rz, zw = lax.fori_loop(0, n_tiles, lambda t, c: image0(own_row(t), True, c), (zero, zero))
    lax.fori_loop(0, 2, lambda t, c: image0(pl.multiple_of(YO - 8 + (cy + 8) * t, 8), False, c), (zero, zero))

    precondition(Y0B, Y1, Z1, 1)

    def image1(t, carry):
        r0 = own_row(t)
        rz1, wz1, zw1, z1w1 = carry

        def use(x, value, total):
            nonlocal rz1, wz1, zw1, z1w1
            w = at(DIAG, x, r0) * value - 0.5 * total
            put(W1, x - XO, r0 - YO, w)
            rz1 = rz1 + at(R, x, r0) * value
            wz1 = wz1 + at(W0, x - XO, r0 - YO) * value
            zw1 = zw1 + at(Z0, x, r0) * w
            z1w1 = z1w1 + value * w

        sweep(Z1, 0, cx, r0, use)
        return rz1, wz1, zw1, z1w1

    rz1, wz1, zw1, z1w1 = lax.fori_loop(0, n_tiles, image1, (zero,) * 4)

    mine = zero
    for q, acc in enumerate((rz, zw, rz1, wz1, zw1, z1w1)):
        mine = jnp.where(sub == q, jnp.sum(acc, axis=0, keepdims=True), mine)
    part[0] = mine
    base = 0
    sent = []
    for s, dims in enumerate(STAGES):
        offs = offsets(dims)
        for n, off in enumerate(offs):
            pltpu.make_async_remote_copy(
                part.at[s], slots.at[base + n], ar_send.at[s], ar_recv.at[s],
                device_id=partner(gx, gy, dims, off), device_id_type=MESH,
            ).start()
        group = slots.at[pl.ds(base, len(offs))]
        both = pltpu.make_async_remote_copy(
            group, group, ar_send.at[s], ar_recv.at[s],
            device_id=partner(gx, gy, dims, offs[0]), device_id_type=MESH,
        )
        both.wait_recv()
        sent.append(both)
        part[s + 1] = part[s] + jnp.sum(slots[base : base + len(offs)], axis=0)
        base += len(offs)
    totals = jnp.sum(part[len(STAGES)], axis=1, keepdims=True)
    rz, zw, rz1, wz1, zw1, z1w1 = [totals[q : q + 1] for q in range(6)]
    step0 = rz / zw
    next_rz = rz - step0 * (rz1 + zw) + step0 * step0 * wz1
    grow = 1.0 + next_rz / rz
    curve = grow * grow * zw - grow * step0 * (zw1 + wz1) + step0 * step0 * z1w1
    step1 = next_rz / curve
    g0 = jnp.broadcast_to(step0 + step1 * grow, (8, nz))
    g1 = jnp.broadcast_to(step1 * step0, (8, nz))

    def finish(x, carry):
        for t in range(n_tiles):
            r0 = YO + 8 * t
            z0, z1 = at(Z0, x, r0), at(Z1, x, r0)
            w0, w1 = at(W0, x - XO, r0 - YO), at(W1, x - XO, r0 - YO)
            put(W0, x - XO, r0 - YO, g0 * z0 - g1 * z1)
            put(W1, x - XO, r0 - YO, at(R, x, r0) - g0 * w0 + g1 * w1)
        pltpu.make_async_copy(W0.at[x], sol_hbm.at[x], out_sem.at[0]).start()
        pltpu.make_async_copy(W1.at[x], res_hbm.at[x], out_sem.at[1]).start()
        return carry

    lax.fori_loop(0, cx, finish, 0)
    pltpu.make_async_copy(W0, sol_hbm, out_sem.at[0]).wait()
    pltpu.make_async_copy(W1, res_hbm, out_sem.at[1]).wait()
    for both in sent:
        both.wait_send()
    for k, (dx, dy) in enumerate(NEAR):

        @pl.when(here(dx, dy))
        def _():
            for copy in halo_copies(k, dx, dy):
                copy.wait_send()


def shards(right_side, conductivity):
    cx, cy, nz = right_side.shape
    ext = pltpu.VMEM((cx + 2 * KW, cy + 2 * YO, nz), jnp.float32)
    own = pltpu.VMEM((cx, cy, nz), jnp.float32)
    dma = pltpu.SemaphoreType.DMA
    any_space = pl.BlockSpec(memory_space=pl.ANY)
    out = jax.ShapeDtypeStruct((cx, cy, nz), jnp.float32)
    return pl.pallas_call(
        kernel,
        out_shape=(out, out),
        in_specs=[any_space, any_space],
        out_specs=(any_space, any_space),
        scratch_shapes=[ext] * 12 + [own] * 2
        + [
            pltpu.VMEM((len(STAGES) + 1, 8, nz), jnp.float32),
            pltpu.VMEM((N_SLOTS, 8, nz), jnp.float32),
            dma((2,)), dma((2,)), dma((16,)), dma((16,)), dma((len(STAGES),)), dma((len(STAGES),)),
        ],
        compiler_params=pltpu.CompilerParams(
            collective_id=0, has_side_effects=True, vmem_limit_bytes=48 << 20
        ),
    )(right_side, conductivity)


def solution(mesh):
    spec = P("gx", "gy", None)
    return jax.shard_map(
        shards, mesh=mesh, in_specs=(spec, spec), out_specs=(spec, spec), check_vma=False
    )
```

time: 305 us -> 68.5 us (0.22)
  blocking collectives: 103 us -> 0 us
  starting transfers between devices: 100 us -> 0 us
  Pallas kernels: 0 us -> 63.1 us
  waiting for transfers between devices: 55.4 us -> 0 us
  other arithmetic: 28 us -> 0 us
  between operations: 8.22 us -> 0.65 us
  local copies, waits for them, and re-layouts: 7.58 us -> 4.38 us
    psum x1 -> x0, blocking collectives: 103 us -> none  [shards(): dots = lax.psum(jnp.stack([jnp.sum(a * b) for a, b in pairs]), ('gx', 'gy'))]
    ppermute x28 -> x0, starting transfers between devices: 100 us -> none  [the longest x10 46.3 us: with_halo(): lax.ppermute(lax.slice_in_dim(block, block.shape[dim] - width, None, axis...]
    pallas_call x0 -> x1, Pallas kernels: none -> 63.1 us  [shards(): pl.pallas_call(kernel, out_shape=(out, out), in_specs=[any_space, any_spa...]
    ppermute x28 -> x0, waiting for transfers between devices: 55.4 us -> none  [the longest x8 27.7 us: from_behind(): return lax.ppermute(x, axis, pairs)]
    add x5 -> x0, other arithmetic: 11.2 us -> none  [the longest x4 7.89 us: chebyshev(): answer = answer + update]
    mul x17 -> x0, other arithmetic: 7.64 us -> none  [the longest x4 2.96 us: local_apply(): face_z * field[:, :, 1:]]
    unnamed x8 -> x6, local copies, waits for them, and re-layouts: 0.23 us -> 4.38 us
    reduce_sum x1 -> x0, other arithmetic: 4.1 us -> none  [shards(): dots = lax.psum(jnp.stack([jnp.sum(a * b) for a, b in pairs]), ('gx', 'gy'))]
  transfers between devices with their start and end apart: 28 -> 0, of which waited for: 12 -> 0; matrix products, arithmetic and copies ran while one was open for 1% -> 0% of each run, Pallas kernels for 0% -> 0%
where the time goes in v2:
time: 68.5 us; the launch traced here: 68.1 us
  Pallas kernels  63.1 us (92%)
  local copies, waits for them, and re-layouts  4.38 us (6%)
    pallas_call x1, Pallas kernels, shards(): pl.pallas_call(kernel, out_shape=(out, out), in_specs=[any_space, any_spa...  63.1 us
    unnamed x6, local copies, waits for them, and re-layouts  4.38 us

profile of v2, /device:TPU:8, one launch (start us, length us, event | category | flops | bytes accessed | tf_op | source)
XLA Modules:
  0.0 68.1 jit_solution(14082826935889840970)
XLA Ops:
  0.6 0.0 copy-start
  0.6 1.2 %copy-done = f32[16,128,128]{2,1,0:T(8,128)S(1)} copy-done((f32[16,128,128]{2,1,0:T(8,128)S(1)}, f32[16,128,128]{2,1,0:T(8,128)}, u32[]{:S(2)}) %copy-start) | copy-done | bytes 1048600
  1.9 0.0 copy-start.1
  1.9 1.2 %copy-done.1 = f32[16,128,128]{2,1,0:T(8,128)S(1)} copy-done((f32[16,128,128]{2,1,0:T(8,128)S(1)}, f32[16,128,128]{2,1,0:T(8,128)}, u32[]{:S(2)}) %copy-start.1) | copy-done | bytes 1048600
  3.1 63.1 %shard_map.41 = (f32[16,128,128]{2,1,0:T(8,128)S(1)}, f32[16,128,128]{2,1,0:T(8,128)S(1)}) custom-call(f32[16,128,128]{2,1,0:T(8,128)S(1)} %copy-done, f32[16,128,128]{2,1,0:T(8,128)S(1)} %copy-done.1), custom_call_target="tpu_custom_call" | custom-call | tf_op jit(solution)/shard_map/pallas_call | solution.py:450
  66.2 1.0 %copy.6 = f32[16,128,128]{2,1,0:T(8,128)} copy(f32[16,128,128]{2,1,0:T(8,128)S(1)} %get-tuple-element.4) | data formatting | bytes 2097152
  67.2 1.0 %copy.7 = f32[16,128,128]{2,1,0:T(8,128)} copy(f32[16,128,128]{2,1,0:T(8,128)S(1)} %get-tuple-element.5) | data formatting | bytes 2097152
Async XLA Ops:
  0.6 1.2 %copy-start = (f32[16,128,128]{2,1,0:T(8,128)S(1)}, f32[16,128,128]{2,1,0:T(8,128)}, u32[]{:S(2)}) copy-start(f32[16,128,128]{2,1,0:T(8,128)} %r_hbm.1) | copy-start | bytes 3145732
  1.9 1.2 %copy-start.1 = (f32[16,128,128]{2,1,0:T(8,128)S(1)}, f32[16,128,128]{2,1,0:T(8,128)}, u32[]{:S(2)}) copy-start(f32[16,128,128]{2,1,0:T(8,128)} %k_hbm.1) | copy-start | bytes 3145732

commit v3 on v2

--- a/solution.py
+++ b/solution.py
@@ -50,33 +50,19 @@
 
 
 def kernel(
-    r_hbm, k_hbm, sol_hbm, res_hbm,
+    r_hbm, k_hbm, sol, res,
     K, R, INV, DIAG, FX, FY, FZ, Y0, Y1, Y0B, Z0, Z1, W0, W1, part, slots,
-    load_sem, out_sem, send_sem, recv_sem, ar_send, ar_recv,
+    load_sem, send_sem, recv_sem, ar_send, ar_recv,
 ):
     cx, cy, nz = r_hbm.shape
     n_gx, n_gy = lax.axis_size("gx"), lax.axis_size("gy")
     gx, gy = lax.axis_index("gx"), lax.axis_index("gy")
-    n_tiles = cy // 8
+    full, brick = cy + 16, cy
+    strip = 48 if full % 48 == 0 else 8
+    own_strip = 64 if brick % 64 == 0 else 8
 
     def here(dx, dy):
         return (gx + dx >= 0) & (gx + dx < n_gx) & (gy + dy >= 0) & (gy + dy < n_gy)
-
-    barrier = pltpu.get_barrier_semaphore()
-    count = 0
-    for dx, dy in NEAR:
-        count = count + here(dx, dy).astype(jnp.int32)
-
-        @pl.when(here(dx, dy))
-        def _():
-            pl.semaphore_signal(barrier, inc=1, device_id=(gx + dx, gy + dy), device_id_type=MESH)
-
-    for dims in STAGES:
-        for off in offsets(dims):
-            pl.semaphore_signal(
-                barrier, inc=1, device_id=partner(gx, gy, dims, off), device_id_type=MESH
-            )
-            count = count + 1
 
     own = (pl.ds(XO, cx), pl.ds(YO, cy))
     loads = [
@@ -85,6 +71,23 @@
     ]
     for load in loads:
         load.start()
+
+    barrier = pltpu.get_barrier_semaphore()
+    count = 0
+    for dx, dy in NEAR:
+        count = count + here(dx, dy).astype(jnp.int32)
+
+        @pl.when(here(dx, dy))
+        def _():
+            pl.semaphore_signal(barrier, inc=1, device_id=(gx + dx, gy + dy), device_id_type=MESH)
+
+    for dims in STAGES:
+        for off in offsets(dims):
+            pl.semaphore_signal(
+                barrier, inc=1, device_id=partner(gx, gy, dims, off), device_id_type=MESH
+            )
+            count = count + 1
+
     pl.semaphore_wait(barrier, count)
 
     def halo_copies(k, dx, dy):
@@ -163,7 +166,8 @@
             K[x, pl.ds(YO + cy, 8)] = jnp.broadcast_to(K[x, pl.ds(YO + cy - 1, 1)], (8, nz))
             R[x, pl.ds(YO + cy, 8)] = flat(8)
 
-    lane = lax.broadcasted_iota(jnp.int32, (8, nz), 1)
+    lane = lax.broadcasted_iota(jnp.int32, (strip, nz), 1)
+    line = lax.broadcasted_iota(jnp.int32, (strip, nz), 0)
     sub = lax.broadcasted_iota(jnp.int32, (8, nz), 0)
     first_lane, last_lane = lane == 0, lane == nz - 1
     one = jnp.float32(1.0)
@@ -173,17 +177,19 @@
     n_lo = jnp.where(has_lo, one, 0.0)
     n_hi = jnp.where(has_hi, one, 0.0)
 
-    def at(ref, x, row):
-        return ref[x + XO, pl.ds(row, 8), :]
+    def at(ref, x, row, h=strip):
+        return ref[x + XO, pl.ds(row, h), :]
 
     def put(ref, x, row, value):
-        ref[x + XO, pl.ds(row, 8), :] = value
-
-    def tile_row(t):
-        return pl.multiple_of(YO - 8 + 8 * t, 8)
-
-    def coefficients(t, carry):
-        r0 = tile_row(t)
+        ref[x + XO, pl.ds(row, value.shape[0]), :] = value
+
+    def strip_row(t):
+        return pl.multiple_of(YO - 8 + strip * t, 8)
+
+    def strips(body):
+        lax.fori_loop(0, full // strip, lambda t, c: body(strip_row(t), c), 0)
+
+    def coefficients(r0, carry):
         low, mid = at(K, -RW - 1, r0), at(K, -RW, r0)
         for x in range(-RW, cx + RW):
             high = at(K, x + 1, r0)
@@ -201,7 +207,7 @@
             low, mid = mid, high
         return carry
 
-    lax.fori_loop(0, n_tiles + 2, coefficients, 0)
+    strips(coefficients)
 
     @pl.when(gx == 0)
     def _():
@@ -221,13 +227,15 @@
         for x in range(n_layers):
             FY[x, pl.ds(YO + cy - 1, 1)] = flat(1)
 
-    def sweep(src, lo, hi, r0, use):
-        prev, cur, f_prev = at(src, lo - 1, r0), at(src, lo, r0), at(FX, lo - 1, r0)
+    def sweep(src, lo, hi, r0, use, h=strip):
+        prev, cur, f_prev = at(src, lo - 1, r0, h), at(src, lo, r0, h), at(FX, lo - 1, r0, h)
         for x in range(lo, hi):
-            nxt, f = at(src, x + 1, r0), at(FX, x, r0)
-            fz = at(FZ, x, r0)
+            nxt, f = at(src, x + 1, r0, h), at(FX, x, r0, h)
+            fz = at(FZ, x, r0, h)
             total = f * nxt + f_prev * prev
-            total = total + (at(FY, x, r0) * at(src, x, r0 + 1) + at(FY, x, r0 - 1) * at(src, x, r0 - 1))
+            total = total + (
+                at(FY, x, r0, h) * at(src, x, r0 + 1, h) + at(FY, x, r0 - 1, h) * at(src, x, r0 - 1, h)
+            )
             total = total + (fz * pltpu.roll(cur, nz - 1, 1) + pltpu.roll(fz * cur, 1, 1))
             use(x, cur, total)
             prev, cur, f_prev = cur, nxt, f
@@ -238,34 +246,41 @@
         )
 
     def precondition(y0, y1, z, reach):
-        def first(t, carry):
-            r0 = tile_row(t)
-
+        def first(r0, carry):
             def use(x, value, total):
                 put(y1, x, r0, A1 * value + B1 * (at(INV, x, r0) * total))
 
             sweep(y0, -reach - 1, cx + reach + 1, r0, use)
             return carry
 
-        lax.fori_loop(0, n_tiles + 2, first, 0)
+        strips(first)
 
         edges = [(MARGIN - 1, 1, m_lo), (cx - MARGIN, -1, m_hi)]
         if reach == MARGIN:
             edges += [(-MARGIN, -1, one), (cx + MARGIN - 1, 1, one)]
 
-        def second(t, carry):
-            r0 = tile_row(t)
-            row = sub + (r0 - YO)
+        def counts(r0):
+            row = line + (r0 - YO)
             over = jnp.where(in_overlap(row), one, 0.0)
+            return row, over, 1.0 + over
+
+        def second(r0, carry):
+            _, _, times = counts(r0)
+
+            def use(x, value, total):
+                y2 = A2 * value + A0 * at(y0, x, r0) + B2 * (at(INV, x, r0) * total)
+                weight = 1.0 + m_lo if x < MARGIN else (1.0 + m_hi if x >= cx - MARGIN else one)
+                put(z, x, r0, (weight * times) * y2)
+
+            sweep(y1, -reach, cx + reach, r0, use)
+            return carry
+
+        strips(second)
+
+        def cut_edges(r0, carry):
+            row, over, times = counts(r0)
             pair_up = 1.0 + over * jnp.where(in_overlap(row + 1), one, 0.0)
             pair_down = 1.0 + over * jnp.where(in_overlap(row - 1), one, 0.0)
-            times = 1.0 + over
-            t_lo, t_hi = times * (1.0 + m_lo), times * (1.0 + m_hi)
-            fixes = {}
-
-            def cut(x, value):
-                fixes[x] = value if x not in fixes else fixes[x] + value
-
             for a, d, weight in edges:
                 def face(row0):
                     return at(FX, a if d > 0 else a - 1, row0)
@@ -279,22 +294,14 @@
                     fz * pltpu.roll(e, nz - 1, 1) + pltpu.roll(fz * e, 1, 1)
                 )
                 side = at(FY, a, r0) * (pair_up * e_up) + at(FY, a, r0 - 1) * (pair_down * e_down)
-                cut(a, weight * (times * (A2 * e + B2 * (inv * flow)) + B2 * (inv * side)))
+                fix = times * (A2 * e + B2 * (inv * flow)) + B2 * (inv * side)
+                put(z, a, r0, at(z, a, r0) - weight * fix)
                 inner = at(FX, a - 1 if d > 0 else a, r0)
-                cut(a - d, (weight * B2) * (times * (at(INV, a - d, r0) * (inner * e))))
-
-            def use(x, value, total):
-                y2 = A2 * value + A0 * at(y0, x, r0) + B2 * (at(INV, x, r0) * total)
-                scale = t_lo if x < MARGIN else (t_hi if x >= cx - MARGIN else times)
-                out = scale * y2
-                if x in fixes:
-                    out = out - fixes[x]
-                put(z, x, r0, out)
-
-            sweep(y1, -reach, cx + reach, r0, use)
+                fix = (weight * B2) * (times * (at(INV, a - d, r0) * (inner * e)))
+                put(z, a - d, r0, at(z, a - d, r0) - fix)
             return carry
 
-        lax.fori_loop(0, n_tiles + 2, second, 0)
+        strips(cut_edges)
 
         def over_x(x):
             if -MARGIN <= x < MARGIN:
@@ -320,14 +327,14 @@
                 return fy * up(v) if d > 0 else down(fy * v)
 
             def e_of(x):
-                return jnp.where(edge, B1 * (at(INV, x, r0) * cross(at(FY, x, r0), at(y0, x, r0))), 0.0)
-
-            prev, cur, f_prev = e_of(-reach - 1), e_of(-reach), at(FX, -reach - 1, r0)
+                return jnp.where(edge, B1 * (at(INV, x, r0, 8) * cross(at(FY, x, r0, 8), at(y0, x, r0, 8))), 0.0)
+
+            prev, cur, f_prev = e_of(-reach - 1), e_of(-reach), at(FX, -reach - 1, r0, 8)
             for x in range(-reach, cx + reach):
-                nxt, f = e_of(x + 1), at(FX, x, r0)
-                fy, fz, inv = at(FY, x, r0), at(FZ, x, r0), at(INV, x, r0)
+                nxt, f = e_of(x + 1), at(FX, x, r0, 8)
+                fy, fz, inv = at(FY, x, r0, 8), at(FZ, x, r0, 8), at(INV, x, r0, 8)
                 times = 1.0 + over_x(x)
-                flow = jnp.where(edge, cross(fy, at(y1, x, r0)), 0.0)
+                flow = jnp.where(edge, cross(fy, at(y1, x, r0, 8)), 0.0)
                 flow = flow + jnp.where(inner, cross(fy, cur), 0.0)
                 flow = flow + (fz * pltpu.roll(cur, nz - 1, 1) + pltpu.roll(fz * cur, 1, 1))
                 side = (1.0 + over_x(x) * over_x(x + 1)) * (f * nxt) if x + 1 != MARGIN and x + 1 != cx - MARGIN else f * nxt
@@ -336,56 +343,44 @@
                     if x != MARGIN and x != cx - MARGIN else f_prev * prev
                 )
                 fix = times * (A2 * cur + B2 * (inv * flow)) + B2 * (inv * side)
-                put(z, x, r0, at(z, x, r0) - weight * fix)
+                put(z, x, r0, at(z, x, r0, 8) - weight * fix)
                 prev, cur, f_prev = cur, nxt, f
 
     zero = jnp.zeros((8, nz), jnp.float32)
     precondition(Y0, Y1, Z0, MARGIN)
 
-    def own_row(t):
-        return pl.multiple_of(YO + 8 * t, 8)
-
-    def image0(r0, inside, carry):
-        rz, zw = carry
-
+    def image0(r0, carry):
         def use(x, value, total):
-            nonlocal rz, zw
             half = 0.5 * total
             put(Y0B, x, r0, (value - at(INV, x, r0) * half) * (1.0 / theta))
-            if inside and 0 <= x < cx:
-                w = at(DIAG, x, r0) * value - half
-                put(W0, x - XO, r0 - YO, w)
-                rz = rz + at(R, x, r0) * value
-                zw = zw + value * w
+            if 0 <= x < cx:
+                put(W0, x - XO, r0 - (YO - 8), at(DIAG, x, r0) * value - half)
 
         sweep(Z0, -3, cx + 3, r0, use)
-        return rz, zw
-
-    rz, zw = lax.fori_loop(0, n_tiles, lambda t, c: image0(own_row(t), True, c), (zero, zero))
-    lax.fori_loop(0, 2, lambda t, c: image0(pl.multiple_of(YO - 8 + (cy + 8) * t, 8), False, c), (zero, zero))
-
+        return carry
+
+    strips(image0)
     precondition(Y0B, Y1, Z1, 1)
 
     def image1(t, carry):
-        r0 = own_row(t)
-        rz1, wz1, zw1, z1w1 = carry
+        r0 = pl.multiple_of(YO + own_strip * t, 8)
+        sums = list(carry)
 
         def use(x, value, total):
-            nonlocal rz1, wz1, zw1, z1w1
-            w = at(DIAG, x, r0) * value - 0.5 * total
-            put(W1, x - XO, r0 - YO, w)
-            rz1 = rz1 + at(R, x, r0) * value
-            wz1 = wz1 + at(W0, x - XO, r0 - YO) * value
-            zw1 = zw1 + at(Z0, x, r0) * w
-            z1w1 = z1w1 + value * w
-
-        sweep(Z1, 0, cx, r0, use)
-        return rz1, wz1, zw1, z1w1
-
-    rz1, wz1, zw1, z1w1 = lax.fori_loop(0, n_tiles, image1, (zero,) * 4)
+            w1 = at(DIAG, x, r0, own_strip) * value - 0.5 * total
+            put(W1, x - XO, r0 - YO, w1)
+            r, z0 = at(R, x, r0, own_strip), at(Z0, x, r0, own_strip)
+            w0 = at(W0, x - XO, r0 - (YO - 8), own_strip)
+            for q, (a, b) in enumerate(((r, z0), (z0, w0), (r, value), (w0, value), (z0, w1), (value, w1))):
+                sums[q] = sums[q] + jnp.sum((a * b).reshape(own_strip // 8, 8, nz), axis=0)
+
+        sweep(Z1, 0, cx, r0, use, own_strip)
+        return tuple(sums)
+
+    sums = lax.fori_loop(0, brick // own_strip, image1, (zero,) * 6)
 
     mine = zero
-    for q, acc in enumerate((rz, zw, rz1, wz1, zw1, z1w1)):
+    for q, acc in enumerate(sums):
         mine = jnp.where(sub == q, jnp.sum(acc, axis=0, keepdims=True), mine)
     part[0] = mine
     base = 0
@@ -413,23 +408,18 @@
     grow = 1.0 + next_rz / rz
     curve = grow * grow * zw - grow * step0 * (zw1 + wz1) + step0 * step0 * z1w1
     step1 = next_rz / curve
-    g0 = jnp.broadcast_to(step0 + step1 * grow, (8, nz))
-    g1 = jnp.broadcast_to(step1 * step0, (8, nz))
+    g0, g1 = step0 + step1 * grow, step1 * step0
+    g0 = jnp.broadcast_to(g0, (brick, nz))
+    g1 = jnp.broadcast_to(g1, (brick, nz))
 
     def finish(x, carry):
-        for t in range(n_tiles):
-            r0 = YO + 8 * t
-            z0, z1 = at(Z0, x, r0), at(Z1, x, r0)
-            w0, w1 = at(W0, x - XO, r0 - YO), at(W1, x - XO, r0 - YO)
-            put(W0, x - XO, r0 - YO, g0 * z0 - g1 * z1)
-            put(W1, x - XO, r0 - YO, at(R, x, r0) - g0 * w0 + g1 * w1)
-        pltpu.make_async_copy(W0.at[x], sol_hbm.at[x], out_sem.at[0]).start()
-        pltpu.make_async_copy(W1.at[x], res_hbm.at[x], out_sem.at[1]).start()
+        z0, z1 = at(Z0, x, YO, brick), at(Z1, x, YO, brick)
+        w0, w1 = at(W0, x - XO, 8, brick), at(W1, x - XO, 0, brick)
+        sol[x] = g0 * z0 - g1 * z1
+        res[x] = at(R, x, YO, brick) - g0 * w0 + g1 * w1
         return carry
 
     lax.fori_loop(0, cx, finish, 0)
-    pltpu.make_async_copy(W0, sol_hbm, out_sem.at[0]).wait()
-    pltpu.make_async_copy(W1, res_hbm, out_sem.at[1]).wait()
     for both in sent:
         both.wait_send()
     for k, (dx, dy) in enumerate(NEAR):
@@ -443,23 +433,27 @@
 def shards(right_side, conductivity):
     cx, cy, nz = right_side.shape
     ext = pltpu.VMEM((cx + 2 * KW, cy + 2 * YO, nz), jnp.float32)
-    own = pltpu.VMEM((cx, cy, nz), jnp.float32)
     dma = pltpu.SemaphoreType.DMA
-    any_space = pl.BlockSpec(memory_space=pl.ANY)
+    hbm = pl.BlockSpec(memory_space=pltpu.MemorySpace.HBM)
     out = jax.ShapeDtypeStruct((cx, cy, nz), jnp.float32)
+    right_side, conductivity = (
+        pltpu.with_memory_space_constraint(v, pltpu.MemorySpace.HBM) for v in (right_side, conductivity)
+    )
     return pl.pallas_call(
         kernel,
         out_shape=(out, out),
-        in_specs=[any_space, any_space],
-        out_specs=(any_space, any_space),
-        scratch_shapes=[ext] * 12 + [own] * 2
+        in_specs=[hbm, hbm],
+        out_specs=(pl.BlockSpec(memory_space=pltpu.MemorySpace.VMEM),) * 2,
+        scratch_shapes=[ext] * 12
         + [
+            pltpu.VMEM((cx, cy + 16, nz), jnp.float32),
+            pltpu.VMEM((cx, cy, nz), jnp.float32),
             pltpu.VMEM((len(STAGES) + 1, 8, nz), jnp.float32),
             pltpu.VMEM((N_SLOTS, 8, nz), jnp.float32),
-            dma((2,)), dma((2,)), dma((16,)), dma((16,)), dma((len(STAGES),)), dma((len(STAGES),)),
+            dma((2,)), dma((16,)), dma((16,)), dma((len(STAGES),)), dma((len(STAGES),)),
         ],
         compiler_params=pltpu.CompilerParams(
-            collective_id=0, has_side_effects=True, vmem_limit_bytes=48 << 20
+            collective_id=0, has_side_effects=True, vmem_limit_bytes=40 << 20
         ),
     )(right_side, conductivity)
 

time: 68.5 us -> 54 us (0.79)
  Pallas kernels: 63.1 us -> 51.1 us
  local copies, waits for them, and re-layouts: 4.38 us -> 1.94 us
    pallas_call x1, Pallas kernels: 63.1 us -> 51.1 us  [shards(): pl.pallas_call(kernel, out_shape=(out, out), in_specs=[hbm, hbm], out_spe...]
    unnamed x6 -> x2, local copies, waits for them, and re-layouts: 4.38 us -> 1.94 us
where the time goes in v3:
time: 54 us; the launch traced here: 53.7 us
  Pallas kernels  51.1 us (95%)
  local copies, waits for them, and re-layouts  1.94 us (4%)
  between operations  0.64 us (1%)
    pallas_call x1, Pallas kernels, shards(): pl.pallas_call(kernel, out_shape=(out, out), in_specs=[hbm, hbm], out_spe...  51.1 us
    unnamed x2, local copies, waits for them, and re-layouts  1.94 us

profile of v3, /device:TPU:8, one launch (start us, length us, event | category | flops | bytes accessed | tf_op | source)
XLA Modules:
  0.0 53.7 jit_solution(16313055273230785586)
XLA Ops:
  0.6 51.1 %shard_map.41 = (f32[16,128,128]{2,1,0:T(8,128)S(1)}, f32[16,128,128]{2,1,0:T(8,128)S(1)}) custom-call(f32[16,128,128]{2,1,0:T(8,128)} %r_hbm.1, f32[16,128,128]{2,1,0:T(8,128)} %k_hbm.1), custom_call_target="tpu_custom_call" | custom-call | tf_op jit(solution)/shard_map/pallas_call | solution.py:442
  51.7 1.0 %copy.6 = f32[16,128,128]{2,1,0:T(8,128)} copy(f32[16,128,128]{2,1,0:T(8,128)S(1)} %get-tuple-element.4) | data formatting | bytes 2097152
  52.7 1.0 %copy.7 = f32[16,128,128]{2,1,0:T(8,128)} copy(f32[16,128,128]{2,1,0:T(8,128)S(1)} %get-tuple-element.5) | data formatting | bytes 2097152

commit v4 on v3

--- a/solution.py
+++ b/solution.py
@@ -30,28 +30,47 @@
 YO = 16
 XO = KW
 
-SIZES = dict(c=2, x=4, z=4, y=4, h=2)
-STAGES = (("c",), ("x", "y"), ("z", "h"))
-NEAR = tuple((dx, dy) for dx in (-1, 0, 1) for dy in (-1, 0, 1) if (dx, dy) != (0, 0))
+SIZES = dict(c=2, x=4, y=4, z=8)
+STAGES = (("c",), ("x", "y"), ("z",))
+CORNERS = ((-1, -1), (-1, 1), (1, -1), (1, 1))
+NEAR = CORNERS + ((0, -1), (0, 1), (-1, 0), (1, 0))
 
 
 def offsets(dims):
-    return [o for o in itertools.product(*[range(SIZES[d]) for d in dims]) if any(o)]
+    def hops(off):
+        return sum(min(o, SIZES[d] - o) for d, o in zip(dims, off))
+
+    every = itertools.product(*[range(SIZES[d]) for d in dims])
+    return sorted((off for off in every if any(off)), key=hops, reverse=True)
 
 
 N_SLOTS = sum(len(offsets(dims)) for dims in STAGES)
 
 
 def partner(gx, gy, dims, off):
-    me = dict(c=gx % 2, x=(gx // 2) % 4, z=gx // 8, y=gy % 4, h=gy // 4)
+    me = dict(c=gx % 2, x=(gx // 2) % 4, y=gy % 4, z=gx // 8 + 4 * (gy // 4))
     for d, o in zip(dims, off):
         me[d] = (me[d] + o) % SIZES[d]
-    return (me["z"] * 8 + me["x"] * 2 + me["c"], me["h"] * 4 + me["y"])
+    return ((me["z"] % 4) * 8 + me["x"] * 2 + me["c"], (me["z"] // 4) * 4 + me["y"])
+
+
+def triangle(start, width):
+    out = []
+    for d in range(1, width):
+        out.append((d, start, width - d))
+        start += width - d
+    return out
+
+
+K_CORNER = triangle(0, KW)
+R_CORNER = triangle(sum(n for _, _, n in K_CORNER), RW)
+CORNER_ROWS = 40
+SIDE = KW + RW
 
 
 def kernel(
     r_hbm, k_hbm, sol, res,
-    K, R, INV, DIAG, FX, FY, FZ, Y0, Y1, Y0B, Z0, Z1, W0, W1, part, slots,
+    K, R, INV, DIAG, FX, FY, FZ, Y0, Y1, Y0B, Z0, Z1, W0, W1, side_out, side_in, corner_out, corner_in, part, slots,
     load_sem, send_sem, recv_sem, ar_send, ar_recv,
 ):
     cx, cy, nz = r_hbm.shape
@@ -88,30 +107,43 @@
             )
             count = count + 1
 
+    for load in loads:
+        load.wait()
+
+    def pack(x, carry):
+        for s, (k_row, r_row) in enumerate(((YO, YO), (YO + cy - KW, YO + cy - RW))):
+            side_out[s, pl.ds(SIDE * x, 8)] = K[x + XO, pl.ds(k_row, 8)]
+            side_out[s, pl.ds(SIDE * x + KW, 8)] = R[x + XO, pl.ds(r_row, 8)]
+        return carry
+
+    lax.fori_loop(0, cx, pack, 0)
+    for c, (dx, dy) in enumerate(CORNERS):
+        for ref, parts in ((K, K_CORNER), (R, R_CORNER)):
+            for d, start, n in parts:
+                x = XO + (cx - d if dx > 0 else d - 1)
+                corner_out[c, pl.ds(start, 8)] = ref[x, pl.ds(YO + cy - n if dy > 0 else YO, 8)]
+
     pl.semaphore_wait(barrier, count)
 
     def halo_copies(k, dx, dy):
-        out = []
-        for n, (src, dst, width) in enumerate(((k_hbm, K, KW), (r_hbm, R, RW))):
-            if dx > 0:
-                sx, tx = pl.ds(cx - width, width), pl.ds(XO - width, width)
-            elif dx < 0:
-                sx, tx = pl.ds(0, width), pl.ds(XO + cx, width)
-            else:
-                sx, tx = pl.ds(0, cx), pl.ds(XO, cx)
-            if dy > 0:
-                sy, ty = pl.ds(cy - 8, 8), pl.ds(YO - 8, 8)
-            elif dy < 0:
-                sy, ty = pl.ds(0, 8), pl.ds(YO + cy, 8)
-            else:
-                sy, ty = pl.ds(0, cy), pl.ds(YO, cy)
-            out.append(
-                pltpu.make_async_remote_copy(
-                    src.at[sx, sy], dst.at[tx, ty], send_sem.at[2 * k + n], recv_sem.at[2 * k + n],
-                    device_id=(gx + dx, gy + dy), device_id_type=MESH,
-                )
+        if dx and dy:
+            pairs = [(corner_out.at[k, pl.ds(0, CORNER_ROWS)], corner_in.at[k, pl.ds(8, CORNER_ROWS)])]
+        elif dy:
+            s = (dy + 1) // 2
+            pairs = [(side_out.at[s, pl.ds(0, SIDE * cx)], side_in.at[s, pl.ds(8, SIDE * cx)])]
+        else:
+            pairs = []
+            for src, dst, width in ((k_hbm, K, KW), (r_hbm, R, RW)):
+                sx = cx - width if dx > 0 else 0
+                tx = XO - width if dx > 0 else XO + cx
+                pairs.append((src.at[pl.ds(sx, width)], dst.at[pl.ds(tx, width), pl.ds(YO, cy)]))
+        return [
+            pltpu.make_async_remote_copy(
+                src, dst, send_sem.at[2 * k + n], recv_sem.at[2 * k + n],
+                device_id=(gx + dx, gy + dy), device_id_type=MESH,
             )
-        return out
+            for n, (src, dst) in enumerate(pairs)
+        ]
 
     for k, (dx, dy) in enumerate(NEAR):
 
@@ -135,14 +167,35 @@
             K[x, pl.ds(YO - 8, rows)] = flat(rows)
             R[x, pl.ds(YO - 8, rows)] = flat(rows)
 
-    for load in loads:
-        load.wait()
     for k, (dx, dy) in enumerate(NEAR):
 
         @pl.when(here(-dx, -dy))
         def _():
             for copy in halo_copies(k, dx, dy):
                 copy.wait_recv()
+
+    for s, (dy, k_off, r_off) in enumerate(((-1, 8, 8 + KW), (1, 8 + KW - 8, 8 + SIDE - 8))):
+
+        @pl.when(here(0, -dy))
+        def _():
+            row = YO - 8 if dy > 0 else YO + cy
+
+            def unpack(x, carry):
+                K[x + XO, pl.ds(row, 8)] = side_in[s, pl.ds(SIDE * x + k_off, 8)]
+                R[x + XO, pl.ds(row, 8)] = side_in[s, pl.ds(SIDE * x + r_off, 8)]
+                return carry
+
+            lax.fori_loop(0, cx, unpack, 0)
+
+    for c, (dx, dy) in enumerate(CORNERS):
+
+        @pl.when(here(-dx, -dy))
+        def _():
+            row = YO - 8 if dy > 0 else YO + cy
+            for ref, parts in ((K, K_CORNER), (R, R_CORNER)):
+                for d, start, n in parts:
+                    x = XO + (-d if dx > 0 else cx + d - 1)
+                    ref[x, pl.ds(row, 8)] = corner_in[c, pl.ds(start + (n if dy > 0 else 8), 8)]
 
     @pl.when(gx == 0)
     def _():
@@ -379,10 +432,13 @@
 
     sums = lax.fori_loop(0, brick // own_strip, image1, (zero,) * 6)
 
+    group_of = lax.broadcasted_iota(jnp.int32, (8, nz), 1) // 16
     mine = zero
     for q, acc in enumerate(sums):
         mine = jnp.where(sub == q, jnp.sum(acc, axis=0, keepdims=True), mine)
-    part[0] = mine
+    for shift in (64, 32, 16):
+        mine = mine + pltpu.roll(mine, shift, 1)
+    part[0] = jnp.sum(jnp.where(sub == group_of, mine, 0.0), axis=0, keepdims=True)
     base = 0
     sent = []
     for s, dims in enumerate(STAGES):
@@ -401,7 +457,8 @@
         sent.append(both)
         part[s + 1] = part[s] + jnp.sum(slots[base : base + len(offs)], axis=0)
         base += len(offs)
-    totals = jnp.sum(part[len(STAGES)], axis=1, keepdims=True)
+    totals = jnp.where(sub == group_of, jnp.broadcast_to(part[len(STAGES)], (8, nz)), 0.0)
+    totals = jnp.sum(totals, axis=1, keepdims=True)
     rz, zw, rz1, wz1, zw1, z1w1 = [totals[q : q + 1] for q in range(6)]
     step0 = rz / zw
     next_rz = rz - step0 * (rz1 + zw) + step0 * step0 * wz1
@@ -448,8 +505,12 @@
         + [
             pltpu.VMEM((cx, cy + 16, nz), jnp.float32),
             pltpu.VMEM((cx, cy, nz), jnp.float32),
-            pltpu.VMEM((len(STAGES) + 1, 8, nz), jnp.float32),
-            pltpu.VMEM((N_SLOTS, 8, nz), jnp.float32),
+            pltpu.VMEM((2, SIDE * cx + 8, nz), jnp.float32),
+            pltpu.VMEM((2, SIDE * cx + 16, nz), jnp.float32),
+            pltpu.VMEM((4, CORNER_ROWS + 8, nz), jnp.float32),
+            pltpu.VMEM((4, CORNER_ROWS + 16, nz), jnp.float32),
+            pltpu.VMEM((len(STAGES) + 1, 1, nz), jnp.float32),
+            pltpu.VMEM((N_SLOTS, 1, nz), jnp.float32),
             dma((2,)), dma((16,)), dma((16,)), dma((len(STAGES),)), dma((len(STAGES),)),
         ],
         compiler_params=pltpu.CompilerParams(

time: 54 us -> 50.1 us (0.928)
  Pallas kernels: 51.1 us -> 47.4 us
    pallas_call x1, Pallas kernels: 51.1 us -> 47.4 us  [shards(): pl.pallas_call(kernel, out_shape=(out, out), in_specs=[hbm, hbm], out_spe...]
where the time goes in v4:
time: 50.1 us; the launch traced here: 50 us
  Pallas kernels  47.4 us (95%)
  local copies, waits for them, and re-layouts  1.94 us (4%)
  between operations  0.64 us (1%)
    pallas_call x1, Pallas kernels, shards(): pl.pallas_call(kernel, out_shape=(out, out), in_specs=[hbm, hbm], out_spe...  47.4 us
    unnamed x2, local copies, waits for them, and re-layouts  1.94 us

profile of v4, /device:TPU:8, one launch (start us, length us, event | category | flops | bytes accessed | tf_op | source)
XLA Modules:
  0.0 50.0 jit_solution(10708525624395002993)
XLA Ops:
  0.6 47.4 %shard_map.41 = (f32[16,128,128]{2,1,0:T(8,128)S(1)}, f32[16,128,128]{2,1,0:T(8,128)S(1)}) custom-call(f32[16,128,128]{2,1,0:T(8,128)} %r_hbm.1, f32[16,128,128]{2,1,0:T(8,128)} %k_hbm.1), custom_call_target="tpu_custom_call" | custom-call | tf_op jit(solution)/shard_map/pallas_call | solution.py:499
  48.1 1.0 %copy.6 = f32[16,128,128]{2,1,0:T(8,128)} copy(f32[16,128,128]{2,1,0:T(8,128)S(1)} %get-tuple-element.4) | data formatting | bytes 2097152
  49.0 1.0 %copy.7 = f32[16,128,128]{2,1,0:T(8,128)} copy(f32[16,128,128]{2,1,0:T(8,128)S(1)} %get-tuple-element.5) | data formatting | bytes 2097152

commit v5 on v4

--- a/solution.py
+++ b/solution.py
@@ -145,84 +145,23 @@
             for n, (src, dst) in enumerate(pairs)
         ]
 
-    for k, (dx, dy) in enumerate(NEAR):
-
-        @pl.when(here(dx, dy))
-        def _():
-            for copy in halo_copies(k, dx, dy):
-                copy.start()
-
-    rows = cy + 16
-    flat = lambda n: jnp.zeros((n, nz), jnp.float32)
-
-    @pl.when(gx == 0)
-    def _():
-        for x in range(XO):
-            K[x, pl.ds(YO - 8, rows)] = flat(rows)
-            R[x, pl.ds(YO - 8, rows)] = flat(rows)
-
-    @pl.when(gx == n_gx - 1)
-    def _():
-        for x in range(XO + cx, XO + cx + KW):
-            K[x, pl.ds(YO - 8, rows)] = flat(rows)
-            R[x, pl.ds(YO - 8, rows)] = flat(rows)
-
-    for k, (dx, dy) in enumerate(NEAR):
-
-        @pl.when(here(-dx, -dy))
-        def _():
-            for copy in halo_copies(k, dx, dy):
-                copy.wait_recv()
-
-    for s, (dy, k_off, r_off) in enumerate(((-1, 8, 8 + KW), (1, 8 + KW - 8, 8 + SIDE - 8))):
-
-        @pl.when(here(0, -dy))
-        def _():
-            row = YO - 8 if dy > 0 else YO + cy
-
-            def unpack(x, carry):
-                K[x + XO, pl.ds(row, 8)] = side_in[s, pl.ds(SIDE * x + k_off, 8)]
-                R[x + XO, pl.ds(row, 8)] = side_in[s, pl.ds(SIDE * x + r_off, 8)]
-                return carry
-
-            lax.fori_loop(0, cx, unpack, 0)
-
-    for c, (dx, dy) in enumerate(CORNERS):
-
-        @pl.when(here(-dx, -dy))
-        def _():
-            row = YO - 8 if dy > 0 else YO + cy
-            for ref, parts in ((K, K_CORNER), (R, R_CORNER)):
-                for d, start, n in parts:
-                    x = XO + (-d if dx > 0 else cx + d - 1)
-                    ref[x, pl.ds(row, 8)] = corner_in[c, pl.ds(start + (n if dy > 0 else 8), 8)]
-
-    @pl.when(gx == 0)
-    def _():
-        K[XO - 1, pl.ds(YO - 8, rows)] = K[XO, pl.ds(YO - 8, rows)]
-
-    @pl.when(gx == n_gx - 1)
-    def _():
-        K[XO + cx, pl.ds(YO - 8, rows)] = K[XO + cx - 1, pl.ds(YO - 8, rows)]
-
-    n_layers = cx + 2 * KW
-
-    @pl.when(gy == 0)
-    def _():
-        for x in range(n_layers):
-            K[x, pl.ds(YO - 8, 8)] = jnp.broadcast_to(K[x, pl.ds(YO, 1)], (8, nz))
-            R[x, pl.ds(YO - 8, 8)] = flat(8)
-
-    @pl.when(gy == n_gy - 1)
-    def _():
-        for x in range(n_layers):
-            K[x, pl.ds(YO + cy, 8)] = jnp.broadcast_to(K[x, pl.ds(YO + cy - 1, 1)], (8, nz))
-            R[x, pl.ds(YO + cy, 8)] = flat(8)
-
-    lane = lax.broadcasted_iota(jnp.int32, (strip, nz), 1)
-    line = lax.broadcasted_iota(jnp.int32, (strip, nz), 0)
+    def send(along_x):
+        for k, (dx, dy) in enumerate(NEAR):
+            if along_x == (dy == 0):
+
+                @pl.when(here(dx, dy))
+                def _():
+                    for copy in halo_copies(k, dx, dy):
+                        copy.start()
+
+    send(False)
+    send(True)
+
     sub = lax.broadcasted_iota(jnp.int32, (8, nz), 0)
-    first_lane, last_lane = lane == 0, lane == nz - 1
+
+    def line_of(h):
+        return lax.broadcasted_iota(jnp.int32, (h, nz), 0)
+
     one = jnp.float32(1.0)
     m_lo = jnp.where(gx > 0, one, 0.0)
     m_hi = jnp.where(gx < n_gx - 1, one, 0.0)
@@ -242,43 +181,49 @@
     def strips(body):
         lax.fori_loop(0, full // strip, lambda t, c: body(strip_row(t), c), 0)
 
-    def coefficients(r0, carry):
-        low, mid = at(K, -RW - 1, r0), at(K, -RW, r0)
-        for x in range(-RW, cx + RW):
-            high = at(K, x + 1, r0)
-            up, down = at(K, x, r0 + 1), at(K, x, r0 - 1)
+    core, tall = cy - 16, 64 if cy % 64 == 0 else 8
+    core_strip = 56 if core % 56 == 0 else 8
+
+    def inside(stage, m):
+        def body(t, carry):
+            stage(pl.multiple_of(YO + tall * t, 8), m, cx - m, tall)
+            return carry
+
+        lax.fori_loop(0, cy // tall, body, 0)
+
+    def around(stage, m, reach):
+        def sides(t, carry):
+            r0 = pl.multiple_of(YO + 8 + core_strip * t, 8)
+            stage(r0, -reach, m, core_strip)
+            stage(r0, cx - m, cx + reach, core_strip)
+            return carry
+
+        def ends(t, carry):
+            stage(pl.multiple_of(YO - 8 + cy * t, 8), -reach, cx + reach, 16)
+            return carry
+
+        lax.fori_loop(0, core // core_strip, sides, 0)
+        lax.fori_loop(0, 2, ends, 0)
+
+    def coefficients(r0, lo, hi, h):
+        lane = lax.broadcasted_iota(jnp.int32, (h, nz), 1)
+        first_lane, last_lane = lane == 0, lane == nz - 1
+        low, mid = at(K, lo - 1, r0, h), at(K, lo, r0, h)
+        for x in range(lo, hi):
+            high = at(K, x + 1, r0, h)
+            up, down = at(K, x, r0 + 1, h), at(K, x, r0 - 1, h)
             right = jnp.where(last_lane, mid, pltpu.roll(mid, nz - 1, 1))
             left = jnp.where(first_lane, mid, pltpu.roll(mid, 1, 1))
             diag = (absorb + 3.0 * mid) + 0.5 * ((low + high) + (up + down) + (left + right))
             inv = 1.0 / diag
-            put(DIAG, x, r0, diag)
+            if 0 <= x < cx:
+                put(DIAG, x, r0, diag)
             put(INV, x, r0, inv)
             put(FX, x, r0, mid + high)
             put(FY, x, r0, mid + up)
             put(FZ, x, r0, jnp.where(last_lane, 0.0, mid + right))
-            put(Y0, x, r0, at(R, x, r0) * (inv * (1.0 / theta)))
+            put(Y0, x, r0, at(R, x, r0, h) * (inv * (1.0 / theta)))
             low, mid = mid, high
-        return carry
-
-    strips(coefficients)
-
-    @pl.when(gx == 0)
-    def _():
-        FX[XO - 1, pl.ds(YO - 8, rows)] = flat(rows)
-
-    @pl.when(gx == n_gx - 1)
-    def _():
-        FX[XO + cx - 1, pl.ds(YO - 8, rows)] = flat(rows)
-
-    @pl.when(gy == 0)
-    def _():
-        for x in range(n_layers):
-            FY[x, pl.ds(YO - 1, 1)] = flat(1)
-
-    @pl.when(gy == n_gy - 1)
-    def _():
-        for x in range(n_layers):
-            FY[x, pl.ds(YO + cy - 1, 1)] = flat(1)
 
     def sweep(src, lo, hi, r0, use, h=strip):
         prev, cur, f_prev = at(src, lo - 1, r0, h), at(src, lo, r0, h), at(FX, lo - 1, r0, h)
@@ -298,40 +243,139 @@
             (row >= cy - MARGIN) & (row < cy + MARGIN) & has_hi
         )
 
+    def counts(r0, h):
+        row = line_of(h) + (r0 - YO)
+        over = jnp.where(in_overlap(row), one, 0.0)
+        return row, over, 1.0 + over
+
+    def first(y0, y1):
+        def stage(r0, lo, hi, h):
+            def use(x, value, total):
+                put(y1, x, r0, A1 * value + B1 * (at(INV, x, r0, h) * total))
+
+            sweep(y0, lo, hi, r0, use, h)
+
+        return stage
+
+    def second(y0, y1, z):
+        def stage(r0, lo, hi, h):
+            _, _, times = counts(r0, h)
+
+            def use(x, value, total):
+                y2 = A2 * value + A0 * at(y0, x, r0, h) + B2 * (at(INV, x, r0, h) * total)
+                weight = 1.0 + m_lo if x < MARGIN else (1.0 + m_hi if x >= cx - MARGIN else one)
+                put(z, x, r0, (weight * times) * y2)
+
+            sweep(y1, lo, hi, r0, use, h)
+
+        return stage
+
+    inside(coefficients, 1)
+    inside(first(Y0, Y1), 2)
+    inside(second(Y0, Y1, Z0), 3)
+
+    rows = cy + 16
+    flat = lambda n: jnp.zeros((n, nz), jnp.float32)
+
+    @pl.when(gx == 0)
+    def _():
+        for x in range(XO):
+            K[x, pl.ds(YO - 8, rows)] = flat(rows)
+            R[x, pl.ds(YO - 8, rows)] = flat(rows)
+
+    @pl.when(gx == n_gx - 1)
+    def _():
+        for x in range(XO + cx, XO + cx + KW):
+            K[x, pl.ds(YO - 8, rows)] = flat(rows)
+            R[x, pl.ds(YO - 8, rows)] = flat(rows)
+
+    for k, (dx, dy) in enumerate(NEAR):
+
+        @pl.when(here(-dx, -dy))
+        def _():
+            for copy in halo_copies(k, dx, dy):
+                copy.wait_recv()
+
+    for s, (dy, k_off, r_off) in enumerate(((-1, 8, 8 + KW), (1, 8 + KW - 8, 8 + SIDE - 8))):
+
+        @pl.when(here(0, -dy))
+        def _():
+            row = YO - 8 if dy > 0 else YO + cy
+
+            def unpack(x, carry):
+                K[x + XO, pl.ds(row, 8)] = side_in[s, pl.ds(SIDE * x + k_off, 8)]
+                R[x + XO, pl.ds(row, 8)] = side_in[s, pl.ds(SIDE * x + r_off, 8)]
+                return carry
+
+            lax.fori_loop(0, cx, unpack, 0)
+
+    for c, (dx, dy) in enumerate(CORNERS):
+
+        @pl.when(here(-dx, -dy))
+        def _():
+            row = YO - 8 if dy > 0 else YO + cy
+            for ref, parts in ((K, K_CORNER), (R, R_CORNER)):
+                for d, start, n in parts:
+                    x = XO + (-d if dx > 0 else cx + d - 1)
+                    ref[x, pl.ds(row, 8)] = corner_in[c, pl.ds(start + (n if dy > 0 else 8), 8)]
+
+    @pl.when(gx == 0)
+    def _():
+        K[XO - 1, pl.ds(YO - 8, rows)] = K[XO, pl.ds(YO - 8, rows)]
+
+    @pl.when(gx == n_gx - 1)
+    def _():
+        K[XO + cx, pl.ds(YO - 8, rows)] = K[XO + cx - 1, pl.ds(YO - 8, rows)]
+
+    n_layers = cx + 2 * KW
+
+    @pl.when(gy == 0)
+    def _():
+        for x in range(n_layers):
+            K[x, pl.ds(YO - 8, 8)] = jnp.broadcast_to(K[x, pl.ds(YO, 1)], (8, nz))
+            R[x, pl.ds(YO - 8, 8)] = flat(8)
+
+    @pl.when(gy == n_gy - 1)
+    def _():
+        for x in range(n_layers):
+            K[x, pl.ds(YO + cy, 8)] = jnp.broadcast_to(K[x, pl.ds(YO + cy - 1, 1)], (8, nz))
+            R[x, pl.ds(YO + cy, 8)] = flat(8)
+
+    around(coefficients, 1, RW)
+
+    @pl.when(gx == 0)
+    def _():
+        FX[XO - 1, pl.ds(YO - 8, rows)] = flat(rows)
+
+    @pl.when(gx == n_gx - 1)
+    def _():
+        FX[XO + cx - 1, pl.ds(YO - 8, rows)] = flat(rows)
+
+    @pl.when(gy == 0)
+    def _():
+        for x in range(n_layers):
+            FY[x, pl.ds(YO - 1, 1)] = flat(1)
+
+    @pl.when(gy == n_gy - 1)
+    def _():
+        for x in range(n_layers):
+            FY[x, pl.ds(YO + cy - 1, 1)] = flat(1)
+
+    around(first(Y0, Y1), 2, MARGIN + 1)
+    around(second(Y0, Y1, Z0), 3, MARGIN)
+
     def precondition(y0, y1, z, reach):
-        def first(r0, carry):
-            def use(x, value, total):
-                put(y1, x, r0, A1 * value + B1 * (at(INV, x, r0) * total))
-
-            sweep(y0, -reach - 1, cx + reach + 1, r0, use)
-            return carry
-
-        strips(first)
-
+        strips(lambda r0, c: (first(y0, y1)(r0, -reach - 1, cx + reach + 1, strip), c)[1])
+        strips(lambda r0, c: (second(y0, y1, z)(r0, -reach, cx + reach, strip), c)[1])
+        cut(y0, y1, z, reach)
+
+    def cut(y0, y1, z, reach):
         edges = [(MARGIN - 1, 1, m_lo), (cx - MARGIN, -1, m_hi)]
         if reach == MARGIN:
             edges += [(-MARGIN, -1, one), (cx + MARGIN - 1, 1, one)]
 
-        def counts(r0):
-            row = line + (r0 - YO)
-            over = jnp.where(in_overlap(row), one, 0.0)
-            return row, over, 1.0 + over
-
-        def second(r0, carry):
-            _, _, times = counts(r0)
-
-            def use(x, value, total):
-                y2 = A2 * value + A0 * at(y0, x, r0) + B2 * (at(INV, x, r0) * total)
-                weight = 1.0 + m_lo if x < MARGIN else (1.0 + m_hi if x >= cx - MARGIN else one)
-                put(z, x, r0, (weight * times) * y2)
-
-            sweep(y1, -reach, cx + reach, r0, use)
-            return carry
-
-        strips(second)
-
         def cut_edges(r0, carry):
-            row, over, times = counts(r0)
+            row, over, times = counts(r0, strip)
             pair_up = 1.0 + over * jnp.where(in_overlap(row + 1), one, 0.0)
             pair_down = 1.0 + over * jnp.where(in_overlap(row - 1), one, 0.0)
             for a, d, weight in edges:
@@ -400,7 +444,7 @@
                 prev, cur, f_prev = cur, nxt, f
 
     zero = jnp.zeros((8, nz), jnp.float32)
-    precondition(Y0, Y1, Z0, MARGIN)
+    cut(Y0, Y1, Z0, MARGIN)
 
     def image0(r0, carry):
         def use(x, value, total):

time: 50.1 us -> 49 us (0.978)
  Pallas kernels: 47.4 us -> 46.4 us
    pallas_call x1, Pallas kernels: 47.4 us -> 46.4 us  [shards(): pl.pallas_call(kernel, out_shape=(out, out), in_specs=[hbm, hbm], out_spe...]
where the time goes in v5:
time: 49 us; the launch traced here: 48.9 us
  Pallas kernels  46.4 us (95%)
  local copies, waits for them, and re-layouts  1.94 us (4%)
  between operations  0.64 us (1%)
    pallas_call x1, Pallas kernels, shards(): pl.pallas_call(kernel, out_shape=(out, out), in_specs=[hbm, hbm], out_spe...  46.4 us
    unnamed x2, local copies, waits for them, and re-layouts  1.94 us

profile of v5, /device:TPU:8, one launch (start us, length us, event | category | flops | bytes accessed | tf_op | source)
XLA Modules:
  0.0 48.9 jit_solution(14893500363321189831)
XLA Ops:
  0.6 46.4 %shard_map.41 = (f32[16,128,128]{2,1,0:T(8,128)S(1)}, f32[16,128,128]{2,1,0:T(8,128)S(1)}) custom-call(f32[16,128,128]{2,1,0:T(8,128)} %r_hbm.1, f32[16,128,128]{2,1,0:T(8,128)} %k_hbm.1), custom_call_target="tpu_custom_call" | custom-call | tf_op jit(solution)/shard_map/pallas_call | solution.py:543
  47.0 1.0 %copy.6 = f32[16,128,128]{2,1,0:T(8,128)} copy(f32[16,128,128]{2,1,0:T(8,128)S(1)} %get-tuple-element.4) | data formatting | bytes 2097152
  48.0 1.0 %copy.7 = f32[16,128,128]{2,1,0:T(8,128)} copy(f32[16,128,128]{2,1,0:T(8,128)S(1)} %get-tuple-element.5) | data formatting | bytes 2097152

commit v6 on v5

--- a/solution.py
+++ b/solution.py
@@ -83,10 +83,13 @@
     def here(dx, dy):
         return (gx + dx >= 0) & (gx + dx < n_gx) & (gy + dy >= 0) & (gy + dy < n_gy)
 
-    own = (pl.ds(XO, cx), pl.ds(YO, cy))
+    piece = cx // 4
     loads = [
-        pltpu.make_async_copy(k_hbm, K.at[own], load_sem.at[0]),
-        pltpu.make_async_copy(r_hbm, R.at[own], load_sem.at[1]),
+        pltpu.make_async_copy(
+            src.at[pl.ds(x, piece)], dst.at[pl.ds(XO + x, piece), pl.ds(YO, cy)], load_sem.at[n, x // piece]
+        )
+        for n, (src, dst) in enumerate(((k_hbm, K), (r_hbm, R)))
+        for x in range(0, cx, piece)
     ]
     for load in loads:
         load.start()
@@ -222,8 +225,11 @@
             put(FX, x, r0, mid + high)
             put(FY, x, r0, mid + up)
             put(FZ, x, r0, jnp.where(last_lane, 0.0, mid + right))
-            put(Y0, x, r0, at(R, x, r0, h) * (inv * (1.0 / theta)))
             low, mid = mid, high
+
+    def start(r0, lo, hi, h):
+        for x in range(lo, hi):
+            put(Y0, x, r0, at(R, x, r0, h) * (at(INV, x, r0, h) * (1.0 / theta)))
 
     def sweep(src, lo, hi, r0, use, h=strip):
         prev, cur, f_prev = at(src, lo - 1, r0, h), at(src, lo, r0, h), at(FX, lo - 1, r0, h)
@@ -271,6 +277,7 @@
         return stage
 
     inside(coefficients, 1)
+    inside(start, 1)
     inside(first(Y0, Y1), 2)
     inside(second(Y0, Y1, Z0), 3)
 
@@ -293,7 +300,7 @@
 
         @pl.when(here(-dx, -dy))
         def _():
-            for copy in halo_copies(k, dx, dy):
+            for copy in halo_copies(k, dx, dy)[: 1 if dy == 0 else 2]:
                 copy.wait_recv()
 
     for s, (dy, k_off, r_off) in enumerate(((-1, 8, 8 + KW), (1, 8 + KW - 8, 8 + SIDE - 8))):
@@ -342,6 +349,15 @@
             R[x, pl.ds(YO + cy, 8)] = flat(8)
 
     around(coefficients, 1, RW)
+
+    for k, (dx, dy) in enumerate(NEAR):
+        if dy == 0:
+
+            @pl.when(here(-dx, -dy))
+            def _():
+                halo_copies(k, dx, dy)[1].wait_recv()
+
+    around(start, 1, RW)
 
     @pl.when(gx == 0)
     def _():
@@ -555,7 +571,7 @@
             pltpu.VMEM((4, CORNER_ROWS + 16, nz), jnp.float32),
             pltpu.VMEM((len(STAGES) + 1, 1, nz), jnp.float32),
             pltpu.VMEM((N_SLOTS, 1, nz), jnp.float32),
-            dma((2,)), dma((16,)), dma((16,)), dma((len(STAGES),)), dma((len(STAGES),)),
+            dma((2, 4)), dma((16,)), dma((16,)), dma((len(STAGES),)), dma((len(STAGES),)),
         ],
         compiler_params=pltpu.CompilerParams(
             collective_id=0, has_side_effects=True, vmem_limit_bytes=40 << 20

time: 49 us -> 48 us (0.980)
  Pallas kernels: 46.4 us -> 45.3 us
    pallas_call x1, Pallas kernels: 46.4 us -> 45.3 us  [shards(): pl.pallas_call(kernel, out_shape=(out, out), in_specs=[hbm, hbm], out_spe...]
where the time goes in v6:
time: 48 us; the launch traced here: 47.9 us
  Pallas kernels  45.3 us (94%)
  local copies, waits for them, and re-layouts  1.94 us (4%)
  between operations  0.64 us (1%)
    pallas_call x1, Pallas kernels, shards(): pl.pallas_call(kernel, out_shape=(out, out), in_specs=[hbm, hbm], out_spe...  45.3 us
    unnamed x2, local copies, waits for them, and re-layouts  1.94 us

profile of v6, /device:TPU:8, one launch (start us, length us, event | category | flops | bytes accessed | tf_op | source)
XLA Modules:
  0.0 47.9 jit_solution(13270296528959610495)
XLA Ops:
  0.6 45.3 %shard_map.41 = (f32[16,128,128]{2,1,0:T(8,128)S(1)}, f32[16,128,128]{2,1,0:T(8,128)S(1)}) custom-call(f32[16,128,128]{2,1,0:T(8,128)} %r_hbm.1, f32[16,128,128]{2,1,0:T(8,128)} %k_hbm.1), custom_call_target="tpu_custom_call" | custom-call | tf_op jit(solution)/shard_map/pallas_call | solution.py:559
  46.0 1.0 %copy.6 = f32[16,128,128]{2,1,0:T(8,128)} copy(f32[16,128,128]{2,1,0:T(8,128)S(1)} %get-tuple-element.4) | data formatting | bytes 2097152
  46.9 1.0 %copy.7 = f32[16,128,128]{2,1,0:T(8,128)} copy(f32[16,128,128]{2,1,0:T(8,128)S(1)} %get-tuple-element.5) | data formatting | bytes 2097152

commit v7 on v6

--- a/solution.py
+++ b/solution.py
@@ -148,17 +148,17 @@
             for n, (src, dst) in enumerate(pairs)
         ]
 
-    def send(along_x):
+    def send(along_x, which):
         for k, (dx, dy) in enumerate(NEAR):
             if along_x == (dy == 0):
 
                 @pl.when(here(dx, dy))
                 def _():
-                    for copy in halo_copies(k, dx, dy):
-                        copy.start()
-
-    send(False)
-    send(True)
+                    halo_copies(k, dx, dy)[which].start()
+
+    send(False, 0)
+    send(True, 0)
+    send(True, 1)
 
     sub = lax.broadcasted_iota(jnp.int32, (8, nz), 0)
 
@@ -184,8 +184,7 @@
     def strips(body):
         lax.fori_loop(0, full // strip, lambda t, c: body(strip_row(t), c), 0)
 
-    core, tall = cy - 16, 64 if cy % 64 == 0 else 8
-    core_strip = 56 if core % 56 == 0 else 8
+    tall = 64 if cy % 64 == 0 else 8
 
     def inside(stage, m):
         def body(t, carry):
@@ -194,19 +193,20 @@
 
         lax.fori_loop(0, cy // tall, body, 0)
 
-    def around(stage, m, reach):
-        def sides(t, carry):
-            r0 = pl.multiple_of(YO + 8 + core_strip * t, 8)
-            stage(r0, -reach, m, core_strip)
-            stage(r0, cx - m, cx + reach, core_strip)
+    def ends(stage, m):
+        def body(t, carry):
+            stage(pl.multiple_of(YO - 8 + cy * t, 8), m, cx - m, 16)
             return carry
 
-        def ends(t, carry):
-            stage(pl.multiple_of(YO - 8 + cy * t, 8), -reach, cx + reach, 16)
+        lax.fori_loop(0, 2, body, 0)
+
+    def sides(stage, m, reach):
+        def body(r0, carry):
+            stage(r0, -reach, m, strip)
+            stage(r0, cx - m, cx + reach, strip)
             return carry
 
-        lax.fori_loop(0, core // core_strip, sides, 0)
-        lax.fori_loop(0, 2, ends, 0)
+        strips(body)
 
     def coefficients(r0, lo, hi, h):
         lane = lax.broadcasted_iota(jnp.int32, (h, nz), 1)
@@ -296,12 +296,16 @@
             K[x, pl.ds(YO - 8, rows)] = flat(rows)
             R[x, pl.ds(YO - 8, rows)] = flat(rows)
 
-    for k, (dx, dy) in enumerate(NEAR):
-
-        @pl.when(here(-dx, -dy))
-        def _():
-            for copy in halo_copies(k, dx, dy)[: 1 if dy == 0 else 2]:
-                copy.wait_recv()
+
+    def receive(along_x, which):
+        for k, (dx, dy) in enumerate(NEAR):
+            if along_x == (dy == 0):
+
+                @pl.when(here(-dx, -dy))
+                def _():
+                    halo_copies(k, dx, dy)[which].wait_recv()
+
+    receive(False, 0)
 
     for s, (dy, k_off, r_off) in enumerate(((-1, 8, 8 + KW), (1, 8 + KW - 8, 8 + SIDE - 8))):
 
@@ -326,6 +330,42 @@
                     x = XO + (-d if dx > 0 else cx + d - 1)
                     ref[x, pl.ds(row, 8)] = corner_in[c, pl.ds(start + (n if dy > 0 else 8), 8)]
 
+    own_layers = tuple(range(XO, XO + cx))
+    halo_layers = tuple(range(XO)) + tuple(range(XO + cx, cx + 2 * KW))
+
+    def mirror(layers):
+        @pl.when(gy == 0)
+        def _():
+            for x in layers:
+                K[x, pl.ds(YO - 8, 8)] = jnp.broadcast_to(K[x, pl.ds(YO, 1)], (8, nz))
+                R[x, pl.ds(YO - 8, 8)] = flat(8)
+
+        @pl.when(gy == n_gy - 1)
+        def _():
+            for x in layers:
+                K[x, pl.ds(YO + cy, 8)] = jnp.broadcast_to(K[x, pl.ds(YO + cy - 1, 1)], (8, nz))
+                R[x, pl.ds(YO + cy, 8)] = flat(8)
+
+    def cut_faces(layers):
+        @pl.when(gy == 0)
+        def _():
+            for x in layers:
+                FY[x, pl.ds(YO - 1, 1)] = flat(1)
+
+        @pl.when(gy == n_gy - 1)
+        def _():
+            for x in layers:
+                FY[x, pl.ds(YO + cy - 1, 1)] = flat(1)
+
+    mirror(own_layers)
+    ends(coefficients, 1)
+    ends(start, 1)
+    cut_faces(own_layers)
+    ends(first(Y0, Y1), 2)
+    ends(second(Y0, Y1, Z0), 3)
+
+    receive(True, 0)
+
     @pl.when(gx == 0)
     def _():
         K[XO - 1, pl.ds(YO - 8, rows)] = K[XO, pl.ds(YO - 8, rows)]
@@ -334,30 +374,11 @@
     def _():
         K[XO + cx, pl.ds(YO - 8, rows)] = K[XO + cx - 1, pl.ds(YO - 8, rows)]
 
-    n_layers = cx + 2 * KW
-
-    @pl.when(gy == 0)
-    def _():
-        for x in range(n_layers):
-            K[x, pl.ds(YO - 8, 8)] = jnp.broadcast_to(K[x, pl.ds(YO, 1)], (8, nz))
-            R[x, pl.ds(YO - 8, 8)] = flat(8)
-
-    @pl.when(gy == n_gy - 1)
-    def _():
-        for x in range(n_layers):
-            K[x, pl.ds(YO + cy, 8)] = jnp.broadcast_to(K[x, pl.ds(YO + cy - 1, 1)], (8, nz))
-            R[x, pl.ds(YO + cy, 8)] = flat(8)
-
-    around(coefficients, 1, RW)
-
-    for k, (dx, dy) in enumerate(NEAR):
-        if dy == 0:
-
-            @pl.when(here(-dx, -dy))
-            def _():
-                halo_copies(k, dx, dy)[1].wait_recv()
-
-    around(start, 1, RW)
+    mirror(halo_layers)
+    sides(coefficients, 1, RW)
+
+    receive(True, 1)
+    sides(start, 1, RW)
 
     @pl.when(gx == 0)
     def _():
@@ -367,18 +388,9 @@
     def _():
         FX[XO + cx - 1, pl.ds(YO - 8, rows)] = flat(rows)
 
-    @pl.when(gy == 0)
-    def _():
-        for x in range(n_layers):
-            FY[x, pl.ds(YO - 1, 1)] = flat(1)
-
-    @pl.when(gy == n_gy - 1)
-    def _():
-        for x in range(n_layers):
-            FY[x, pl.ds(YO + cy - 1, 1)] = flat(1)
-
-    around(first(Y0, Y1), 2, MARGIN + 1)
-    around(second(Y0, Y1, Z0), 3, MARGIN)
+    cut_faces(halo_layers + (XO, XO + cx - 1))
+    sides(first(Y0, Y1), 2, MARGIN + 1)
+    sides(second(Y0, Y1, Z0), 3, MARGIN)
 
     def precondition(y0, y1, z, reach):
         strips(lambda r0, c: (first(y0, y1)(r0, -reach - 1, cx + reach + 1, strip), c)[1])

time: 48 us -> 47.6 us (level)
  no operation moved by 1% of the time
where the time goes in v7:
time: 47.6 us; the launch traced here: 47.5 us
  Pallas kernels  44.9 us (94%)
  local copies, waits for them, and re-layouts  1.94 us (4%)
  between operations  0.64 us (1%)
    pallas_call x1, Pallas kernels, shards(): pl.pallas_call(kernel, out_shape=(out, out), in_specs=[hbm, hbm], out_spe...  44.9 us
    unnamed x2, local copies, waits for them, and re-layouts  1.94 us

profile of v7, /device:TPU:8, one launch (start us, length us, event | category | flops | bytes accessed | tf_op | source)
XLA Modules:
  0.0 47.5 jit_solution(15950529430703211082)
XLA Ops:
  0.6 44.9 %shard_map.41 = (f32[16,128,128]{2,1,0:T(8,128)S(1)}, f32[16,128,128]{2,1,0:T(8,128)S(1)}) custom-call(f32[16,128,128]{2,1,0:T(8,128)} %r_hbm.1, f32[16,128,128]{2,1,0:T(8,128)} %k_hbm.1), custom_call_target="tpu_custom_call" | custom-call | tf_op jit(solution)/shard_map/pallas_call | solution.py:571
  45.5 1.0 %copy.6 = f32[16,128,128]{2,1,0:T(8,128)} copy(f32[16,128,128]{2,1,0:T(8,128)S(1)} %get-tuple-element.4) | data formatting | bytes 2097152
  46.5 1.0 %copy.7 = f32[16,128,128]{2,1,0:T(8,128)} copy(f32[16,128,128]{2,1,0:T(8,128)S(1)} %get-tuple-element.5) | data formatting | bytes 2097152

commit v8 on v7

--- a/solution.py
+++ b/solution.py
@@ -364,33 +364,54 @@
     ends(first(Y0, Y1), 2)
     ends(second(Y0, Y1, Z0), 3)
 
-    receive(True, 0)
-
-    @pl.when(gx == 0)
-    def _():
-        K[XO - 1, pl.ds(YO - 8, rows)] = K[XO, pl.ds(YO - 8, rows)]
-
-    @pl.when(gx == n_gx - 1)
-    def _():
-        K[XO + cx, pl.ds(YO - 8, rows)] = K[XO + cx - 1, pl.ds(YO - 8, rows)]
-
-    mirror(halo_layers)
-    sides(coefficients, 1, RW)
-
-    receive(True, 1)
-    sides(start, 1, RW)
-
-    @pl.when(gx == 0)
-    def _():
-        FX[XO - 1, pl.ds(YO - 8, rows)] = flat(rows)
-
-    @pl.when(gx == n_gx - 1)
-    def _():
-        FX[XO + cx - 1, pl.ds(YO - 8, rows)] = flat(rows)
-
-    cut_faces(halo_layers + (XO, XO + cx - 1))
-    sides(first(Y0, Y1), 2, MARGIN + 1)
-    sides(second(Y0, Y1, Z0), 3, MARGIN)
+    def take(dx, which):
+        k = NEAR.index((dx, 0))
+
+        @pl.when(here(-dx, 0))
+        def _():
+            halo_copies(k, dx, 0)[which].wait_recv()
+
+    def side_of(dx):
+        halo = tuple(range(XO)) if dx > 0 else tuple(range(XO + cx, cx + 2 * KW))
+        edge, outer = (XO, XO - 1) if dx > 0 else (XO + cx - 1, XO + cx)
+        at_end = gx == 0 if dx > 0 else gx == n_gx - 1
+
+        def run(stage, m, reach):
+            def body(r0, carry):
+                if dx > 0:
+                    stage(r0, -reach, m, strip)
+                else:
+                    stage(r0, cx - m, cx + reach, strip)
+                return carry
+
+            strips(body)
+
+        take(dx, 0)
+
+        @pl.when(at_end)
+        def _():
+            K[outer, pl.ds(YO - 8, rows)] = K[edge, pl.ds(YO - 8, rows)]
+
+        mirror(halo)
+        run(coefficients, 1, RW)
+        take(dx, 1)
+        run(start, 1, RW)
+
+        @pl.when(at_end)
+        def _():
+            FX[min(edge, outer), pl.ds(YO - 8, rows)] = flat(rows)
+
+        cut_faces(halo + (edge,))
+        run(first(Y0, Y1), 2, MARGIN + 1)
+        run(second(Y0, Y1, Z0), 3, MARGIN)
+
+    even = gx % 2 == 0
+    for turn in (True, False):
+        for dx in (-1, 1):
+
+            @pl.when(even == (turn == (dx < 0)))
+            def _():
+                side_of(dx)
 
     def precondition(y0, y1, z, reach):
         strips(lambda r0, c: (first(y0, y1)(r0, -reach - 1, cx + reach + 1, strip), c)[1])

time: 47.6 us -> 46.9 us (0.985)
  Pallas kernels: 44.9 us -> 44.2 us
    pallas_call x1, Pallas kernels: 44.9 us -> 44.2 us  [shards(): pl.pallas_call(kernel, out_shape=(out, out), in_specs=[hbm, hbm], out_spe...]
where the time goes in v8:
time: 46.9 us; the launch traced here: 46.8 us
  Pallas kernels  44.2 us (94%)
  local copies, waits for them, and re-layouts  1.94 us (4%)
  between operations  0.64 us (1%)
    pallas_call x1, Pallas kernels, shards(): pl.pallas_call(kernel, out_shape=(out, out), in_specs=[hbm, hbm], out_spe...  44.2 us
    unnamed x2, local copies, waits for them, and re-layouts  1.94 us

profile of v8, /device:TPU:8, one launch (start us, length us, event | category | flops | bytes accessed | tf_op | source)
XLA Modules:
  0.0 46.8 jit_solution(15842693216908020491)
XLA Ops:
  0.6 44.2 %shard_map.41 = (f32[16,128,128]{2,1,0:T(8,128)S(1)}, f32[16,128,128]{2,1,0:T(8,128)S(1)}) custom-call(f32[16,128,128]{2,1,0:T(8,128)} %r_hbm.1, f32[16,128,128]{2,1,0:T(8,128)} %k_hbm.1), custom_call_target="tpu_custom_call" | custom-call | tf_op jit(solution)/shard_map/pallas_call | solution.py:592
  44.8 1.0 %copy.6 = f32[16,128,128]{2,1,0:T(8,128)} copy(f32[16,128,128]{2,1,0:T(8,128)S(1)} %get-tuple-element.4) | data formatting | bytes 2097152
  45.8 1.0 %copy.7 = f32[16,128,128]{2,1,0:T(8,128)} copy(f32[16,128,128]{2,1,0:T(8,128)S(1)} %get-tuple-element.5) | data formatting | bytes 2097152
